TPU v7x, 256 devices: a whole 4x4x8 slice. The times are simulated.
256 devices in a mesh: row: 16 (over z, x_lo), col: 16 (over y, x_hi, core).
Axes of the slice: x: 4 (x_hi: 2, x_lo: 2; x = x_hi * 2 + x_lo), y: 4, z: 8, core: 2. Of those that a mesh axis runs over, the one named last changes fastest.
Arguments:
- corner: bfloat16 [16, 16, 64, 64], P('row', 'col'), may hold values from -0.75 to 0.75
- top_edge: bfloat16 [16, 16, 64, 1024], P('row', 'col'), may hold values from -0.75 to 0.75
- left_edge: bfloat16 [16, 16, 64, 1024], P('row', 'col'), may hold values from -0.75 to 0.75
- site_tensor: bfloat16 [16, 16, 2, 4, 4, 4, 4], P('row', 'col'), may hold values from -1.3984375 to 1.3984375
- sketch: bfloat16 [16, 16, 64, 1024], P('row', 'col'), may hold values from -0.1875 to 0.1875
- grad_left: bfloat16 [16, 16, 64, 1024], P('row', 'col'), may hold values from -0.019897461 to 0.019897461
- grad_top: bfloat16 [16, 16, 64, 1024], P('row', 'col'), may hold values from -0.019897461 to 0.019897461
Outputs:
- corner_grad: bfloat16 [16, 16, 64, 64], P('row', 'col')
- top_grad: bfloat16 [16, 16, 64, 1024], P('row', 'col')
- left_grad: bfloat16 [16, 16, 64, 1024], P('row', 'col')
- site_grad: float32 [16, 16, 2, 4, 4, 4, 4], P('row', 'col')
All inputs are finite; a program needn't handle non-finite values.
Results may differ from a plain program's by a relative error of at most 0.014.
Values may be sent and summed in bfloat16 or wider, within the bound.
No kernel may reach another device: no remote copies, remote signals or barrier semaphores. Data moves between devices by JAX's collectives and lax.ppermute only.
A program may use at most 64 MiB of HBM per device.

v0:
```python
import jax
import jax.numpy as jnp
from jax import lax
from jax.sharding import PartitionSpec as P


def from_behind(value, axis, by):
    length = lax.axis_size(axis)
    return lax.ppermute(value, axis, [(i, (i + by) % length) for i in range(length)])


def local(corner, top_edge, left_edge, site_tensor, sketch, grad_left, grad_top):
    own_corner = corner[0, 0]
    own_top = top_edge[0, 0]
    own_left = left_edge[0, 0]
    tensor_site = site_tensor[0, 0]
    own_sketch = sketch[0, 0]
    own_gleft = grad_left[0, 0]
    own_gtop = grad_top[0, 0]
    env_dim = own_corner.shape[0]
    bond_dim = tensor_site.shape[1]
    leg_dim = bond_dim * bond_dim
    order_total = leg_dim * env_dim
    block_len = min(env_dim, 32)
    block_count = env_dim // block_len
    corner_above, top_used = from_behind((own_corner, own_top), "row", 1)
    corner_used, left_used = from_behind((corner_above, own_left), "col", 1)
    first_prod = jnp.dot(corner_used, top_used, preferred_element_type=jnp.float32).astype(
        jnp.bfloat16
    )
    left_three = left_used.reshape(env_dim, leg_dim, env_dim)

    def left_block(block_num):
        return left_three[:, :, block_num * block_len : (block_num + 1) * block_len]

    def ket_block(second_prod):
        second_six = second_prod.reshape(bond_dim, bond_dim, block_len, bond_dim, bond_dim, env_dim)
        ket_layer = jnp.einsum(
            "abmcet,pcavs->pbmevst", second_six, tensor_site, preferred_element_type=jnp.float32
        ).astype(jnp.bfloat16)
        return (second_six, ket_layer)

    gleft_three = own_gleft.reshape(env_dim, leg_dim, env_dim)
    kept = []
    sketch_parts = []
    right_parts = []
    downward = jnp.zeros((env_dim, order_total), jnp.float32)
    for block_num in range(block_count):
        second_prod = jnp.einsum(
            "lwm,lx->wmx", left_block(block_num), first_prod, preferred_element_type=jnp.float32
        ).astype(jnp.bfloat16)
        kept.append(second_prod)
        second_six, ket_layer = ket_block(second_prod)
        quad_blk = jnp.einsum(
            "pbmevst,pebxz->szmvxt", ket_layer, tensor_site, preferred_element_type=jnp.float32
        ).astype(jnp.bfloat16)
        quad_blk = quad_blk.reshape(leg_dim * block_len, order_total)
        sketch_parts.append(
            jnp.einsum(
                "kc,rc->kr", own_sketch, quad_blk, preferred_element_type=jnp.float32
            ).reshape(env_dim, leg_dim, block_len)
        )
        right_parts.append(
            jnp.einsum("kc,rc->kr", own_gtop, quad_blk, preferred_element_type=jnp.float32).reshape(
                env_dim, leg_dim, block_len
            )
        )
        rows_left = gleft_three[:, :, block_num * block_len : (block_num + 1) * block_len].reshape(
            env_dim, leg_dim * block_len
        )
        downward = downward + jnp.dot(rows_left, quad_blk, preferred_element_type=jnp.float32)
    sketched = (
        jnp.concatenate(sketch_parts, axis=2).reshape(env_dim, order_total).astype(jnp.bfloat16)
    )
    rightward = (
        jnp.concatenate(right_parts, axis=2).reshape(env_dim, order_total).astype(jnp.bfloat16)
    )
    sketch_below = from_behind(sketched, "row", -1)
    sketch_beside = from_behind(sketched, "col", -1)
    from_above = from_behind(downward.astype(jnp.bfloat16), "row", 1)
    from_left = from_behind(rightward, "col", 1)
    arrived = (from_above.astype(jnp.float32) + from_left.astype(jnp.float32)).astype(jnp.bfloat16)
    left_factor = jnp.concatenate([own_gleft, sketch_beside, arrived], axis=0).reshape(
        3 * env_dim, leg_dim, env_dim
    )
    right_factor = jnp.concatenate([sketch_below, own_gtop, own_sketch], axis=0)
    grad_first = jnp.zeros((env_dim, order_total), jnp.float32)
    bra_part = jnp.zeros(tensor_site.shape, jnp.float32)
    ket_part = jnp.zeros(tensor_site.shape, jnp.float32)
    left_parts = []
    for block_num in range(block_count):
        left_piece = left_block(block_num)
        second_prod = kept[block_num]
        second_six, ket_layer = ket_block(second_prod)
        factor_rows = left_factor[
            :, :, block_num * block_len : (block_num + 1) * block_len
        ].reshape(3 * env_dim, leg_dim * block_len)
        grad_quad = jnp.einsum(
            "kr,kc->rc", factor_rows, right_factor, preferred_element_type=jnp.float32
        ).astype(jnp.bfloat16)
        grad_quad = grad_quad.reshape(bond_dim, bond_dim, block_len, bond_dim, bond_dim, env_dim)
        grad_ket = jnp.einsum(
            "szmvxt,pebxz->pbmevst", grad_quad, tensor_site, preferred_element_type=jnp.float32
        ).astype(jnp.bfloat16)
        bra_part = bra_part + jnp.einsum(
            "pbmevst,szmvxt->pebxz", ket_layer, grad_quad, preferred_element_type=jnp.float32
        )
        grad_second = jnp.einsum(
            "pbmevst,pcavs->abmcet", grad_ket, tensor_site, preferred_element_type=jnp.float32
        ).astype(jnp.bfloat16)
        ket_part = ket_part + jnp.einsum(
            "abmcet,pbmevst->pcavs", second_six, grad_ket, preferred_element_type=jnp.float32
        )
        grad_mat = grad_second.reshape(leg_dim, block_len, order_total)
        grad_first = grad_first + jnp.einsum(
            "lwm,wmx->lx", left_piece, grad_mat, preferred_element_type=jnp.float32
        )
        left_parts.append(
            jnp.einsum(
                "lx,wmx->lwm", first_prod, grad_mat, preferred_element_type=jnp.float32
            ).astype(jnp.bfloat16)
        )
    grad_lefted = jnp.concatenate(left_parts, axis=2).reshape(env_dim, order_total)
    grad_first = grad_first.astype(jnp.bfloat16)
    grad_topped = jnp.einsum(
        "lt,lx->tx", corner_used, grad_first, preferred_element_type=jnp.float32
    ).astype(jnp.bfloat16)
    grad_cornered = jnp.einsum(
        "lx,tx->lt", grad_first, top_used, preferred_element_type=jnp.float32
    ).astype(jnp.bfloat16)
    top_result, corner_mid = from_behind((grad_topped, grad_cornered), "row", -1)
    left_result, corner_result = from_behind((grad_lefted, corner_mid), "col", -1)
    site_result = ket_part + bra_part
    return (
        corner_result[None, None],
        top_result[None, None],
        left_result[None, None],
        site_result[None, None],
    )


def solution(mesh):
    in_specs = (
        P("row", "col", None, None),
        P("row", "col", None, None),
        P("row", "col", None, None),
        P("row", "col", None, None, None, None, None),
        P("row", "col", None, None),
        P("row", "col", None, None),
        P("row", "col", None, None),
    )
    out_specs = (
        P("row", "col", None, None),
        P("row", "col", None, None),
        P("row", "col", None, None),
        P("row", "col", None, None, None, None, None),
    )
    return jax.shard_map(local, mesh=mesh, in_specs=in_specs, out_specs=out_specs, check_vma=False)
```

profile of v0, /device:TPU:1, one launch (start us, length us, event | category | flops | bytes accessed | tf_op | source)
XLA Modules:
  0.0 198.0 jit_solution(14136040265239573778)
XLA Ops:
  0.6 2.1 %collective-permute-start = (bf16[64,64]{1,0:T(8,128)(2,1)}, bf16[64,64]{1,0:T(8,128)(2,1)S(1)}, u32[]{:S(2)}, u32[]{:S(2)}) collective-permute-start(bf16[64,64]{1,0:T(8,128)(2,1)} %bitcast.278), channel_id=1, source_target_pairs={{0,16},{16,32},{32,48},{48,64},{64,80},{80,96},{96,112},{112,128},... | collective-permute-start | bytes 24584 | tf_op jit(solution)/shard_map/ppermute | solution.py:9
  2.7 1.6 collective-permute-start.2
  4.3 3.9 %collective-permute-start.3 = (bf16[64,1024]{1,0:T(8,128)(2,1)}, bf16[64,1024]{1,0:T(8,128)(2,1)S(1)}, u32[]{:S(2)}, u32[]{:S(2)}) collective-permute-start(bf16[64,1024]{1,0:T(8,128)(2,1)} %bitcast.276), channel_id=1, source_target_pairs={{0,1},{1,2},{2,3},{3,4},{4,5},{5,6},{6,7},{7,8},{8,9},{9,10},{10,1... | collective-permute-start | bytes 393224 | tf_op jit(solution)/shard_map/ppermute | solution.py:9
  10.0 1.7 copy.99
  11.7 1.7 copy.96
  13.3 1.7 copy.87
  15.0 1.7 copy.84
  19.2 2.3 %reshape.81 = bf16[4,4,32,4,4,64]{5,4,3,2,1,0:T(4,128)(2,1)} reshape(bf16[16,32,1024]{2,1,0:T(8,128)(2,1)S(1)} %convert_bitcast_fusion) | data formatting | bytes 2097152 | tf_op jit(solution)/shard_map/reshape | solution.py:37
  23.4 4.1 %fusion.16 = bf16[2,4,32,4,4,4,64,1]{6,5,4,0,3,2,1,7:T(4,128)(2,1)S(1)} fusion(bf16[2,4,4,4,4,1,1,1]{1,4,2,3,0,7,6,5:T(4,128)(2,1)} %copy.84, bf16[4,4,32,4,4,64,1,1]{5,4,3,2,1,0,7,6:T(4,128)(2,1)S(1)} %bitcast.247), kind=kOutput, calls=%fused_computation.24 | convolution fusion | flops 34603008 | bytes 3146752 | tf_op jit(solution)/shard_map/abmcet,pcavs->pbmevst/dot_general | solution.py:38
  27.6 2.7 %fusion.20 = bf16[4,4,32,4,4,64]{5,1,4,0,3,2:T(4,128)(2,1)S(1)} fusion(bf16[2,4,4,4,4,1,1,1]{1,4,0,2,3,7,6,5:T(4,128)(2,1)S(1)} %copy-done.21, bf16[2,4,32,4,4,4,64,1]{6,5,4,0,3,2,1,7:T(4,128)(2,1)S(1)} %fusion.16), kind=kOutput, calls=%fused_computation.28 | convolution fusion | flops 34078720 | bytes 3146752 | tf_op jit(solution)/shard_map/pbmevst,pebxz->szmvxt/dot_general | solution.py:54
  32.7 2.1 %fusion.47 = bf16[64,512]{1,0:T(8,128)(2,1)} fusion(bf16[512,1024]{1,0:T(8,128)(2,1)S(1)} %reshape.79, bf16[1,1,64,1024]{3,2,1,0:T(8,128)(2,1)} %param.13), kind=kOutput, calls=%fused_computation.60 | convolution fusion | flops 67141632 | bytes 1245184 | tf_op jit(solution)/shard_map/kc,rc->kr/dot_general | solution.py:64
  34.9 1.6 copy.55
  36.5 2.0 %fusion.45 = bf16[64,512]{1,0:T(8,128)(2,1)} fusion(bf16[512,1024]{1,0:T(8,128)(2,1)S(1)} %reshape.79, bf16[1,1,64,1024]{3,2,1,0:T(8,128)(2,1)} %param.11), kind=kOutput, calls=%fused_computation.58 | convolution fusion | flops 67141632 | bytes 1245184 | tf_op jit(solution)/shard_map/kc,rc->kr/dot_general | solution.py:59
  38.5 1.9 fusion.102
  40.4 3.3 %fusion.17 = bf16[2,4,32,4,4,4,64,1]{6,5,4,0,3,2,1,7:T(4,128)(2,1)S(1)} fusion(bf16[2,4,4,4,4,1,1,1]{1,4,2,3,0,7,6,5:T(4,128)(2,1)S(1)} %copy-done.23, bf16[4,4,32,4,4,64,1,1]{5,4,3,2,1,0,7,6:T(4,128)(2,1)S(1)} %bitcast.245), kind=kOutput, calls=%fused_computation.25 | convolution fusion | flops 34603008 | bytes 3146752 | tf_op jit(solution)/shard_map/abmcet,pcavs->pbmevst/dot_general | solution.py:38
  43.7 2.7 %fusion.21 = bf16[4,4,32,4,4,64]{5,1,4,0,3,2:T(4,128)(2,1)S(1)} fusion(bf16[2,4,4,4,4,1,1,1]{1,4,0,2,3,7,6,5:T(4,128)(2,1)S(1)} %copy-done.22, bf16[2,4,32,4,4,4,64,1]{6,5,4,0,3,2,1,7:T(4,128)(2,1)S(1)} %fusion.17), kind=kOutput, calls=%fused_computation.29 | convolution fusion | flops 34078720 | bytes 3146752 | tf_op jit(solution)/shard_map/pbmevst,pebxz->szmvxt/dot_general | solution.py:54
  51.5 3.6 %collective-permute-start.6 = (bf16[64,1024]{1,0:T(8,128)(2,1)S(1)}, bf16[64,1024]{1,0:T(8,128)(2,1)S(1)}, u32[]{:S(2)}, u32[]{:S(2)}) collective-permute-start(bf16[64,1024]{1,0:T(8,128)(2,1)S(1)} %copy.135), channel_id=1, source_target_pairs={{0,1},{1,2},{2,3},{3,4},{4,5},{5,6},{6,7},{7,8},{8,9},{9,10},{10,1... | collective-permute-start | bytes 393224 | tf_op jit(solution)/shard_map/ppermute | solution.py:9
  57.7 2.7 %collective-permute-start.7 = (bf16[64,1024]{1,0:T(8,128)(2,1)S(1)}, bf16[64,1024]{1,0:T(8,128)(2,1)S(1)}, u32[]{:S(2)}, u32[]{:S(2)}) collective-permute-start(bf16[64,1024]{1,0:T(8,128)(2,1)S(1)} %copy.60), channel_id=1, source_target_pairs={{0,240},{16,0},{32,16},{48,32},{64,48},{80,64},{96,80},{112,96},{1... | collective-permute-start | bytes 393224 | tf_op jit(solution)/shard_map/ppermute | solution.py:9
  60.4 2.9 %collective-permute-done.5 = bf16[64,1024]{1,0:T(8,128)(2,1)S(1)} collective-permute-done((bf16[64,1024]{1,0:T(8,128)(2,1)S(1)}, bf16[64,1024]{1,0:T(8,128)(2,1)S(1)}, u32[]{:S(2)}, u32[]{:S(2)}) %collective-permute-start.5) | collective-permute-done | bytes 131104 | tf_op jit(solution)/shard_map/ppermute | solution.py:9
  63.5 4.5 %collective-permute-done.4 = bf16[64,1024]{0,1:T(8,128)(2,1)S(1)} collective-permute-done((bf16[64,1024]{0,1:T(8,128)(2,1)S(1)}, bf16[64,1024]{0,1:T(8,128)(2,1)S(1)}, u32[]{:S(2)}, u32[]{:S(2)}) %collective-permute-start.4) | collective-permute-done | bytes 131104 | tf_op jit(solution)/shard_map/ppermute | solution.py:9
  71.5 22.9 %fusion.59 = f32[4,4,2,4,4]{4,1,3,2,0:T(4,128)} fusion(bf16[2,4,32,4,4,4,64,1]{6,5,4,0,3,2,1,7:T(4,128)(2,1)} %copy-done.26, bf16[4,4,32,4,4,64]{5,4,3,2,1,0:T(4,128)(2,1)S(1)} %reshape.89), kind=kOutput, calls=%fused_computation.64 | convolution fusion | flops 33554432 | bytes 3147776 | tf_op jit(solution)/shard_map/pbmevst,szmvxt->pebxz/dot_general | solution.py:105
  94.8 2.3 %reshape.92 = bf16[4,4,32,4,4,64]{5,4,3,2,1,0:T(4,128)(2,1)} reshape(bf16[512,1024]{1,0:T(8,128)(2,1)S(1)} %convolution_convert_fusion) | data formatting | bytes 2097152 | tf_op jit(solution)/shard_map/reshape | solution.py:101
  97.2 23.6 %fusion.64 = f32[4,4,2,4,4]{4,1,3,2,0:T(4,128)} fusion(bf16[2,4,32,4,4,4,64,1]{6,5,4,0,3,2,1,7:T(4,128)(2,1)} %copy-done.27, bf16[4,4,32,4,4,64]{5,4,3,2,1,0:T(4,128)(2,1)} %reshape.92), kind=kOutput, calls=%fused_computation.65 | convolution fusion | flops 33554432 | bytes 3147776 | tf_op jit(solution)/shard_map/pbmevst,szmvxt->pebxz/dot_general | solution.py:105
  120.8 2.7 %fusion.19 = bf16[2,4,32,4,4,4,64,1]{6,1,3,0,4,2,5,7:T(4,128)(2,1)S(1)} fusion(bf16[2,4,4,4,4,1,1,1]{2,3,4,1,0,7,6,5:T(4,128)(2,1)S(1)} %copy-done.17, bf16[4,4,32,4,4,64]{5,4,3,2,1,0:T(4,128)(2,1)S(1)} %copy-done), kind=kOutput, calls=%fused_computation.27 | convolution fusion | flops 34603008 | bytes 3146752 | tf_op jit(solution)/shard_map/szmvxt,pebxz->pbmevst/dot_general | solution.py:102
  123.5 2.7 %fusion.18 = bf16[2,4,32,4,4,4,64,1]{6,1,3,0,4,2,5,7:T(4,128)(2,1)S(1)} fusion(bf16[2,4,4,4,4,1,1,1]{2,3,4,1,0,7,6,5:T(4,128)(2,1)S(1)} %copy-done.17, bf16[4,4,32,4,4,64]{5,4,3,2,1,0:T(4,128)(2,1)S(1)} %reshape.89), kind=kOutput, calls=%fused_computation.26 | convolution fusion | flops 34603008 | bytes 3146752 | tf_op jit(solution)/shard_map/szmvxt,pebxz->pbmevst/dot_general | solution.py:102
  126.6 14.3 %fusion.49 = f32[2,4,4,4,4]{4,2,3,1,0:T(4,128)} fusion(bf16[4,4,32,4,4,64,1,1]{5,4,3,2,1,0,7,6:T(4,128)(2,1)S(1)} %bitcast.248, bf16[2,4,32,4,4,4,64,1]{6,1,3,0,4,2,5,7:T(4,128)(2,1)S(1)} %fusion.18), kind=kOutput, calls=%fused_computation.62 | convolution fusion | flops 33554432 | bytes 3147776 | tf_op jit(solution)/shard_map/abmcet,pbmevst->pcavs/dot_general | solution.py:111
  141.0 5.8 %fusion.22 = bf16[4,4,32,4,4,64]{5,0,3,4,2,1:T(4,128)(2,1)} fusion(bf16[2,4,4,4,4,1,1,1]{3,2,4,0,1,7,6,5:T(4,128)(2,1)S(1)} %copy-done.20, bf16[2,4,32,4,4,4,64,1]{6,1,3,0,4,2,5,7:T(4,128)(2,1)S(1)} %fusion.18), kind=kOutput, calls=%fused_computation.30 | convolution fusion | flops 34078720 | bytes 3146752 | tf_op jit(solution)/shard_map/pbmevst,pcavs->abmcet/dot_general | solution.py:108
  146.7 4.8 %fusion.23 = bf16[4,4,32,4,4,64]{5,0,3,4,2,1:T(4,128)(2,1)S(1)} fusion(bf16[2,4,4,4,4,1,1,1]{3,2,4,0,1,7,6,5:T(4,128)(2,1)S(1)} %copy-done.20, bf16[2,4,32,4,4,4,64,1]{6,1,3,0,4,2,5,7:T(4,128)(2,1)S(1)} %fusion.19), kind=kOutput, calls=%fused_computation.31 | convolution fusion | flops 34078720 | bytes 3146752 | tf_op jit(solution)/shard_map/pbmevst,pcavs->abmcet/dot_general | solution.py:108
  159.1 1.5 fusion.42
  161.9 2.8 %collective-permute-start.8 = (bf16[64,64]{1,0:T(8,128)(2,1)S(1)}, bf16[64,64]{1,0:T(8,128)(2,1)S(1)}, u32[]{:S(2)}, u32[]{:S(2)}) collective-permute-start(bf16[64,64]{1,0:T(8,128)(2,1)S(1)} %convolution_convert_fusion.10), channel_id=1, source_target_pairs={{0,240},{16,0},{32,16},{48,32},{64,48},{80,64},{96,80},{112,96},{1... | collective-permute-start | bytes 24584 | tf_op jit(solution)/shard_map/ppermute | solution.py:9
  167.0 4.9 %collective-permute-start.9 = (bf16[64,64]{1,0:T(8,128)(2,1)S(1)}, bf16[64,64]{1,0:T(8,128)(2,1)S(1)}, u32[]{:S(2)}, u32[]{:S(2)}) collective-permute-start(bf16[64,64]{1,0:T(8,128)(2,1)S(1)} %collective-permute-done.8), channel_id=1, source_target_pairs={{0,15},{1,0},{2,1},{3,2},{4,3},{5,4},{6,5},{7,6},{8,7},{9,8},{10,9... | collective-permute-start | bytes 24584 | tf_op jit(solution)/shard_map/ppermute | solution.py:9
  171.9 22.9 %fusion.84 = f32[1,1,2,4,4,4,4]{3,6,4,5,2,1,0:T(4,128)S(1)} fusion(f32[2,4,4,4,4]{4,2,3,1,0:T(4,128)} %fusion.49, bf16[4,4,32,4,4,64,1,1]{5,4,3,2,1,0,7,6:T(4,128)(2,1)S(1)} %bitcast.246, bf16[2,4,32,4,4,4,64,1]{6,1,3,0,4,2,5,7:T(4,128)(2,1)} %copy-done.1, f32[4,4,2,4,4]{4,1,3,2,0:T(4,128)} %fusion.64, f32[4,4,2,4,4]{4,1,3,2,0:T(4,128)} %fusion.59), kind=kOutput, calls=%fused_computation.69 | convolution fusion | flops 33555968 | bytes 3153920 | tf_op jit(solution)/shard_map/abmcet,pbmevst->pcavs/dot_general | solution.py:111
  (117 shorter events, 34.5 us)
Async XLA Ops:
  0.6 16.1 %collective-permute-start = (bf16[64,64]{1,0:T(8,128)(2,1)}, bf16[64,64]{1,0:T(8,128)(2,1)S(1)}, u32[]{:S(2)}, u32[]{:S(2)}) collective-permute-start(bf16[64,64]{1,0:T(8,128)(2,1)} %bitcast.278), channel_id=1, source_target_pairs={{0,16},{16,32},{32,48},{48,64},{64,80},{80,96},{96,112},{112,128},... | collective-permute-start | bytes 24584 | tf_op jit(solution)/shard_map/ppermute | solution.py:9
  2.7 15.6 %collective-permute-start.2 = (bf16[64,1024]{1,0:T(8,128)(2,1)}, bf16[64,1024]{1,0:T(8,128)(2,1)S(1)}, u32[]{:S(2)}, u32[]{:S(2)}) collective-permute-start(bf16[64,1024]{1,0:T(8,128)(2,1)} %bitcast.277), channel_id=1, source_target_pairs={{0,16},{16,32},{32,48},{48,64},{64,80},{80,96},{96,112},{112,128},... | collective-permute-start | bytes 393224 | tf_op jit(solution)/shard_map/ppermute | solution.py:9
  4.3 12.8 %collective-permute-start.3 = (bf16[64,1024]{1,0:T(8,128)(2,1)}, bf16[64,1024]{1,0:T(8,128)(2,1)S(1)}, u32[]{:S(2)}, u32[]{:S(2)}) collective-permute-start(bf16[64,1024]{1,0:T(8,128)(2,1)} %bitcast.276), channel_id=1, source_target_pairs={{0,1},{1,2},{2,3},{3,4},{4,5},{5,6},{6,7},{7,8},{8,9},{9,10},{10,1... | collective-permute-start | bytes 393224 | tf_op jit(solution)/shard_map/ppermute | solution.py:9
  16.7 1.6 collective-permute-start.1
  23.4 4.1 %copy-start.6 = (bf16[4,4,32,4,4,64]{5,4,3,2,1,0:T(4,128)(2,1)}, bf16[4,4,32,4,4,64]{5,4,3,2,1,0:T(4,128)(2,1)S(1)}, u32[]{:S(2)}) copy-start(bf16[4,4,32,4,4,64]{5,4,3,2,1,0:T(4,128)(2,1)S(1)} %reshape.78) | copy-start | bytes 3145732
  23.4 4.1 %copy-start.21 = (bf16[2,4,4,4,4,1,1,1]{1,4,0,2,3,7,6,5:T(4,128)(2,1)S(1)}, bf16[2,4,4,4,4,1,1,1]{1,4,0,2,3,7,6,5:T(4,128)(2,1)}, u32[]{:S(2)}) copy-start(bf16[2,4,4,4,4,1,1,1]{1,4,0,2,3,7,6,5:T(4,128)(2,1)} %copy.87) | copy-start | bytes 3076
  32.7 7.7 %copy-start.4 = (bf16[4,4,32,4,4,64]{5,4,3,2,1,0:T(4,128)(2,1)S(1)}, bf16[4,4,32,4,4,64]{5,4,3,2,1,0:T(4,128)(2,1)}, u32[]{:S(2)}) copy-start(bf16[4,4,32,4,4,64]{5,4,3,2,1,0:T(4,128)(2,1)} %reshape.81) | copy-start | bytes 3145732
  36.5 3.9 %copy-start.23 = (bf16[2,4,4,4,4,1,1,1]{1,4,2,3,0,7,6,5:T(4,128)(2,1)S(1)}, bf16[2,4,4,4,4,1,1,1]{1,4,2,3,0,7,6,5:T(4,128)(2,1)}, u32[]{:S(2)}) copy-start(bf16[2,4,4,4,4,1,1,1]{1,4,2,3,0,7,6,5:T(4,128)(2,1)} %copy.84) | copy-start | bytes 3076
  40.4 3.3 %copy-start.22 = (bf16[2,4,4,4,4,1,1,1]{1,4,0,2,3,7,6,5:T(4,128)(2,1)S(1)}, bf16[2,4,4,4,4,1,1,1]{1,4,0,2,3,7,6,5:T(4,128)(2,1)}, u32[]{:S(2)}) copy-start(bf16[2,4,4,4,4,1,1,1]{1,4,0,2,3,7,6,5:T(4,128)(2,1)} %copy.87) | copy-start | bytes 3076
  48.9 6.3 %copy-start.9 = (f32[1024,64]{0,1:T(8,128)S(1)}, f32[1024,64]{0,1:T(8,128)}, u32[]{:S(2)}) copy-start(f32[1024,64]{0,1:T(8,128)} %fusion.102) | copy-start | bytes 786436
  48.9 6.2 %copy-start.15 = (bf16[64,16,32]{0,2,1:T(8,128)(2,1)S(1)}, bf16[64,16,32]{0,2,1:T(8,128)(2,1)}, u32[]{:S(2)}) copy-start(bf16[64,16,32]{0,2,1:T(8,128)(2,1)} %get-tuple-element.14) | copy-start | bytes 196612
  48.9 7.1 %copy-start.12 = (bf16[1,1,64,1024]{3,2,1,0:T(8,128)(2,1)S(1)}, bf16[1,1,64,1024]{3,2,1,0:T(8,128)(2,1)}, u32[]{:S(2)}) copy-start(bf16[1,1,64,1024]{3,2,1,0:T(8,128)(2,1)} %param.11) | copy-start | bytes 393220
  50.3 6.2 %copy-start.18 = (bf16[64,512]{1,0:T(8,128)(2,1)S(1)}, bf16[64,512]{1,0:T(8,128)(2,1)}, u32[]{:S(2)}) copy-start(bf16[64,512]{1,0:T(8,128)(2,1)} %fusion.45) | copy-start | bytes 196612
  51.5 8.8 %collective-permute-start.6 = (bf16[64,1024]{1,0:T(8,128)(2,1)S(1)}, bf16[64,1024]{1,0:T(8,128)(2,1)S(1)}, u32[]{:S(2)}, u32[]{:S(2)}) collective-permute-start(bf16[64,1024]{1,0:T(8,128)(2,1)S(1)} %copy.135), channel_id=1, source_target_pairs={{0,1},{1,2},{2,3},{3,4},{4,5},{5,6},{6,7},{7,8},{8,9},{9,10},{10,1... | collective-permute-start | bytes 393224 | tf_op jit(solution)/shard_map/ppermute | solution.py:9
  55.5 7.8 %collective-permute-start.5 = (bf16[64,1024]{1,0:T(8,128)(2,1)S(1)}, bf16[64,1024]{1,0:T(8,128)(2,1)S(1)}, u32[]{:S(2)}, u32[]{:S(2)}) collective-permute-start(bf16[64,1024]{1,0:T(8,128)(2,1)S(1)} %fusion.44), channel_id=1, source_target_pairs={{0,16},{16,32},{32,48},{48,64},{64,80},{80,96},{96,112},{112,128},... | collective-permute-start | bytes 393224 | tf_op jit(solution)/shard_map/ppermute | solution.py:9
  56.6 13.1 %copy-start.10 = (bf16[1,1,64,1024]{3,2,1,0:T(8,128)(2,1)S(1)}, bf16[1,1,64,1024]{3,2,1,0:T(8,128)(2,1)}, u32[]{:S(2)}) copy-start(bf16[1,1,64,1024]{3,2,1,0:T(8,128)(2,1)} %param.13) | copy-start | bytes 393220
  56.9 11.1 %collective-permute-start.4 = (bf16[64,1024]{0,1:T(8,128)(2,1)S(1)}, bf16[64,1024]{0,1:T(8,128)(2,1)S(1)}, u32[]{:S(2)}, u32[]{:S(2)}) collective-permute-start(bf16[64,1024]{0,1:T(8,128)(2,1)S(1)} %bitcast.251), channel_id=1, source_target_pairs={{0,15},{1,0},{2,1},{3,2},{4,3},{5,4},{6,5},{7,6},{8,7},{9,8},{10,9... | collective-permute-start | bytes 393224 | tf_op jit(solution)/shard_map/ppermute | solution.py:9
  57.7 11.3 %collective-permute-start.7 = (bf16[64,1024]{1,0:T(8,128)(2,1)S(1)}, bf16[64,1024]{1,0:T(8,128)(2,1)S(1)}, u32[]{:S(2)}, u32[]{:S(2)}) collective-permute-start(bf16[64,1024]{1,0:T(8,128)(2,1)S(1)} %copy.60), channel_id=1, source_target_pairs={{0,240},{16,0},{32,16},{48,32},{64,48},{80,64},{96,80},{112,96},{1... | collective-permute-start | bytes 393224 | tf_op jit(solution)/shard_map/ppermute | solution.py:9
  71.5 22.9 %copy-start.11 = (bf16[1,1,64,1024]{3,2,1,0:T(8,128)(2,1)S(1)}, bf16[1,1,64,1024]{3,2,1,0:T(8,128)(2,1)}, u32[]{:S(2)}) copy-start(bf16[1,1,64,1024]{3,2,1,0:T(8,128)(2,1)} %param.13) | copy-start | bytes 393220
  71.5 22.9 %copy-start.13 = (bf16[1,1,64,1024]{3,2,1,0:T(8,128)(2,1)S(1)}, bf16[1,1,64,1024]{3,2,1,0:T(8,128)(2,1)}, u32[]{:S(2)}) copy-start(bf16[1,1,64,1024]{3,2,1,0:T(8,128)(2,1)} %param.11) | copy-start | bytes 393220
  71.5 22.9 %copy-start.19 = (bf16[192,16,32]{0,2,1:T(8,128)(2,1)S(1)}, bf16[192,16,32]{0,2,1:T(8,128)(2,1)}, u32[]{:S(2)}) copy-start(bf16[192,16,32]{0,2,1:T(8,128)(2,1)} %get-tuple-element.13) | copy-start | bytes 589828
  71.5 22.9 %copy-start.25 = (bf16[64,1024]{1,0:T(8,128)(2,1)S(1)}, bf16[64,1024]{1,0:T(8,128)(2,1)}, u32[]{:S(2)}) copy-start(bf16[64,1024]{1,0:T(8,128)(2,1)} %copy-done.24) | copy-start | bytes 393220
  97.2 23.6 %copy-start = (bf16[4,4,32,4,4,64]{5,4,3,2,1,0:T(4,128)(2,1)S(1)}, bf16[4,4,32,4,4,64]{5,4,3,2,1,0:T(4,128)(2,1)}, u32[]{:S(2)}) copy-start(bf16[4,4,32,4,4,64]{5,4,3,2,1,0:T(4,128)(2,1)} %reshape.92) | copy-start | bytes 3145732
  97.2 23.6 %copy-start.17 = (bf16[2,4,4,4,4,1,1,1]{2,3,4,1,0,7,6,5:T(4,128)(2,1)S(1)}, bf16[2,4,4,4,4,1,1,1]{2,3,4,1,0,7,6,5:T(4,128)(2,1)}, u32[]{:S(2)}) copy-start(bf16[2,4,4,4,4,1,1,1]{2,3,4,1,0,7,6,5:T(4,128)(2,1)} %copy.96) | copy-start | bytes 3076
  123.5 23.2 %copy-start.1 = (bf16[2,4,32,4,4,4,64,1]{6,1,3,0,4,2,5,7:T(4,128)(2,1)}, bf16[2,4,32,4,4,4,64,1]{6,1,3,0,4,2,5,7:T(4,128)(2,1)S(1)}, u32[]{:S(2)}) copy-start(bf16[2,4,32,4,4,4,64,1]{6,1,3,0,4,2,5,7:T(4,128)(2,1)S(1)} %fusion.19) | copy-start | bytes 6291460
  123.5 3.1 %copy-start.7 = (bf16[4,4,32,4,4,64]{5,4,3,2,1,0:T(4,128)(2,1)S(1)}, bf16[4,4,32,4,4,64]{5,4,3,2,1,0:T(4,128)(2,1)}, u32[]{:S(2)}) copy-start(bf16[4,4,32,4,4,64]{5,4,3,2,1,0:T(4,128)(2,1)} %copy-done.6) | copy-start | bytes 3145732
  126.6 14.3 %copy-start.20 = (bf16[2,4,4,4,4,1,1,1]{3,2,4,0,1,7,6,5:T(4,128)(2,1)S(1)}, bf16[2,4,4,4,4,1,1,1]{3,2,4,0,1,7,6,5:T(4,128)(2,1)}, u32[]{:S(2)}) copy-start(bf16[2,4,4,4,4,1,1,1]{3,2,4,0,1,7,6,5:T(4,128)(2,1)} %copy.99) | copy-start | bytes 3076
  158.7 13.3 %copy-start.5 = (bf16[4,4,32,4,4,64]{5,4,3,2,1,0:T(4,128)(2,1)S(1)}, bf16[4,4,32,4,4,64]{5,4,3,2,1,0:T(4,128)(2,1)}, u32[]{:S(2)}) copy-start(bf16[4,4,32,4,4,64]{5,4,3,2,1,0:T(4,128)(2,1)} %reshape.81) | copy-start | bytes 3145732
  161.9 5.1 %collective-permute-start.8 = (bf16[64,64]{1,0:T(8,128)(2,1)S(1)}, bf16[64,64]{1,0:T(8,128)(2,1)S(1)}, u32[]{:S(2)}, u32[]{:S(2)}) collective-permute-start(bf16[64,64]{1,0:T(8,128)(2,1)S(1)} %convolution_convert_fusion.10), channel_id=1, source_target_pairs={{0,240},{16,0},{32,16},{48,32},{64,48},{80,64},{96,80},{112,96},{1... | collective-permute-start | bytes 24584 | tf_op jit(solution)/shard_map/ppermute | solution.py:9
  164.8 31.1 %collective-permute-start.11 = (bf16[64,1024]{1,0:T(8,128)(2,1)S(1)}, bf16[64,1024]{1,0:T(8,128)(2,1)S(1)}, u32[]{:S(2)}, u32[]{:S(2)}) collective-permute-start(bf16[64,1024]{1,0:T(8,128)(2,1)S(1)} %copy.71), channel_id=1, source_target_pairs={{0,15},{1,0},{2,1},{3,2},{4,3},{5,4},{6,5},{7,6},{8,7},{9,8},{10,9... | collective-permute-start | bytes 393224 | tf_op jit(solution)/shard_map/ppermute | solution.py:9
  165.8 30.1 %collective-permute-start.10 = (bf16[64,1024]{1,0:T(8,128)(2,1)S(1)}, bf16[64,1024]{1,0:T(8,128)(2,1)S(1)}, u32[]{:S(2)}, u32[]{:S(2)}) collective-permute-start(bf16[64,1024]{1,0:T(8,128)(2,1)S(1)} %fusion.43), channel_id=1, source_target_pairs={{0,240},{16,0},{32,16},{48,32},{64,48},{80,64},{96,80},{112,96},{1... | collective-permute-start | bytes 393224 | tf_op jit(solution)/shard_map/ppermute | solution.py:9
  167.0 28.8 %collective-permute-start.9 = (bf16[64,64]{1,0:T(8,128)(2,1)S(1)}, bf16[64,64]{1,0:T(8,128)(2,1)S(1)}, u32[]{:S(2)}, u32[]{:S(2)}) collective-permute-start(bf16[64,64]{1,0:T(8,128)(2,1)S(1)} %collective-permute-done.8), channel_id=1, source_target_pairs={{0,15},{1,0},{2,1},{3,2},{4,3},{5,4},{6,5},{7,6},{8,7},{9,8},{10,9... | collective-permute-start | bytes 24584 | tf_op jit(solution)/shard_map/ppermute | solution.py:9
  (8 other events, 15.1 us)
where the time goes:
time: 202 us; the launch traced here: 198 us
  matrix products  128 us (63%)
  local copies, waits for them, and re-layouts  33.1 us (16%)
  starting transfers between devices  25.4 us (13%)
  waiting for transfers between devices  8.38 us (4%)
    dot_general x2, matrix products, local(): jnp.einsum('pbmevst,szmvxt->pebxz', ket_layer, grad_quad, preferred_eleme...  46.5 us
    dot_general x2, matrix products, local(): jnp.einsum('abmcet,pbmevst->pcavs', second_six, grad_ket, preferred_eleme...  37.3 us
    ppermute x12, starting transfers between devices, from_behind(): lax.ppermute(value, axis, [(i, (i + by) % length) for i in range(length)])  25.4 us
    dot_general x2, matrix products, local(): jnp.einsum('pbmevst,pcavs->abmcet', grad_ket, tensor_site, preferred_elem...  10.5 us
    ppermute x12, waiting for transfers between devices, from_behind(): lax.ppermute(value, axis, [(i, (i + by) % length) for i in range(length)])  8.38 us
    dot_general x2, matrix products, ket_block(): jnp.einsum('abmcet,pcavs->pbmevst', second_six, tensor_site, preferred_el...  7.39 us
    squeeze x4, local copies, waits for them, and re-layouts, local(): tensor_site = site_tensor[0, 0]  6.69 us
    dot_general x2, matrix products, local(): jnp.einsum('pbmevst,pebxz->szmvxt', ket_layer, tensor_site, preferred_ele...  5.47 us
  transfers between devices with their start and end apart: 12, of which 3 were waited for; matrix products, arithmetic and copies ran while one was open for 18% of the time, Pallas kernels for 0%

commit v1 on v0

v1 whole, which is shorter than its diff:
```python
import functools

import jax
import jax.numpy as jnp
from jax import lax
from jax.experimental import pallas as pl
from jax.experimental.pallas import tpu as pltpu
from jax.sharding import PartitionSpec as P

BF = jnp.bfloat16
F32 = jnp.float32
CHI = 64
DD = 16
ORDER = DD * CHI
HALF = CHI // 2
WIDE = 2 * CHI


def dot(lhs, rhs):
    return jnp.dot(lhs, rhs, preferred_element_type=F32)


def dot_nt(lhs, rhs):
    return lax.dot_general(lhs, rhs, (((1,), (1,)), ((), ())), preferred_element_type=F32)


def dot_tn(lhs, rhs):
    return lax.dot_general(lhs, rhs, (((0,), (0,)), ((), ())), preferred_element_type=F32)


def iota(shape, axis):
    return lax.broadcasted_iota(jnp.int32, shape, axis)


def first_half(shape):
    return iota(shape, 1) % WIDE < CHI


def to_rows(nat, rows_ref, out_ref, column):
    value = nat.astype(F32)
    rows_ref[...] = jnp.concatenate([value, value], axis=0).T
    low = first_half((DD, WIDE))
    for at in range(HALF):
        even = rows_ref[pl.ds(2 * at, DD, stride=CHI), :]
        odd = rows_ref[pl.ds(2 * at + 1, DD, stride=CHI), :]
        out_ref[at * DD : (at + 1) * DD, column : column + WIDE] = jnp.where(low, even, odd).astype(BF)


def from_rows(value, rows_ref):
    for at in range(HALF):
        tile = value[at * DD : (at + 1) * DD, :]
        rows_ref[pl.ds(2 * at, DD, stride=CHI), :] = tile
        rows_ref[pl.ds(2 * at + 1, DD, stride=CHI), :] = tile
    turned = rows_ref[...].T
    even = iota((CHI, ORDER), 1) % 2 == 0
    return jnp.where(even, turned[:CHI], turned[CHI:])


def spread(nat, out_ref, row):
    value = nat.astype(F32)
    low = first_half((CHI, WIDE))
    zero = jnp.zeros((CHI, WIDE), F32)
    for pair in range(DD // 2):
        tile = value[:, pair * WIDE : (pair + 1) * WIDE]
        swapped = pltpu.roll(tile, CHI, 1)
        at = 2 * pair * WIDE
        out_ref[row : row + CHI, at : at + WIDE] = jnp.where(low, tile, zero).astype(BF)
        out_ref[row + CHI : row + WIDE, at : at + WIDE] = jnp.where(low, zero, swapped).astype(BF)
        at = at + WIDE
        out_ref[row : row + CHI, at : at + WIDE] = jnp.where(low, swapped, zero).astype(BF)
        out_ref[row + CHI : row + WIDE, at : at + WIDE] = jnp.where(low, zero, tile).astype(BF)


def gather_pair(value):
    low = first_half((CHI, WIDE))
    even, odd = value[:CHI], value[CHI:]
    stay = jnp.where(low, even[:, :WIDE], odd[:, WIDE:])
    move = jnp.where(low, even[:, WIDE:], odd[:, :WIDE])
    return stay + pltpu.roll(move, CHI, 1)


def leg_maps():
    column = iota((DD, 2 * WIDE), 1)
    small = iota((DD, 2 * WIDE), 0)
    ket_c = ((column // 4) % 4) * 4 + column // 64 == small
    bra_c = (column % 4) * 4 + (column // 16) % 4 == small
    return ket_c.astype(BF), bra_c.astype(BF)


def prepare_kernel(site_ref, sketch_ref, gtop_ref, gleft_ref, a_ref, ket_ref, bra_ref, cols_ref, turned_ref, gwide_ref, rows_ref):
    ket_map, bra_map = leg_maps()
    total = None
    for phys in range(2):
        site = site_ref[phys]
        ket = dot_tn(ket_map, dot_tn(site, ket_map).astype(BF))
        bra = dot_tn(bra_map, dot_tn(site, bra_map).astype(BF))
        ket_ref[phys] = ket.astype(BF)
        bra_ref[phys] = bra.astype(BF)
        total = ket * bra if total is None else total + ket * bra
    a_ref[...] = total.astype(BF)
    to_rows(gtop_ref[...], rows_ref, cols_ref, 0)
    to_rows(sketch_ref[...], rows_ref, cols_ref, WIDE)
    turned_ref[...] = cols_ref[...].T
    spread(gleft_ref[...], gwide_ref, 0)


def forward_kernel(
    corner_ref, top_ref, left_ref, a_ref, turned_ref, gwide_ref,
    sketched_ref, downward_ref, rightward_ref, tops_ref, first_ref, lwide_ref, second_ref, rows_ref, quad_ref,
):
    to_rows(top_ref[...], rows_ref, tops_ref, 0)
    corner = corner_ref[...]
    nothing = jnp.zeros((CHI, CHI), BF)
    corner_two = jnp.concatenate(
        [jnp.concatenate([corner, nothing], axis=1), jnp.concatenate([nothing, corner], axis=1)], axis=0
    )
    first_ref[...] = dot_nt(tops_ref[...], corner_two).astype(BF)
    spread(left_ref[...], lwide_ref, 0)

    def second_step(pair, carry):
        at = pl.multiple_of(pair * 2 * WIDE, 2 * WIDE)
        block = dot(first_ref[...], lwide_ref[:, pl.ds(at, 2 * WIDE)]).astype(BF)
        row = pl.multiple_of(pair * 2 * DD, 2 * DD)
        for one in range(HALF):
            piece = block[one * DD : (one + 1) * DD]
            second_ref[pl.ds(row, DD), one * WIDE : (one + 1) * WIDE] = piece[:, :WIDE]
            second_ref[pl.ds(row + DD, DD), one * WIDE : (one + 1) * WIDE] = piece[:, WIDE:]
        return carry

    lax.fori_loop(0, DD // 2, second_step, 0, unroll=2)

    def quad_step(pair, carry):
        at = pl.multiple_of(pair * 2 * WIDE, 2 * WIDE)
        block = dot(a_ref[...], second_ref[:, pl.ds(at, 2 * WIDE)]).astype(BF)
        row = pl.multiple_of(pair * 2 * DD, 2 * DD)
        for leg in range(DD):
            piece = block[leg * DD : (leg + 1) * DD]
            quad_ref[pl.ds(row, DD), leg * WIDE : (leg + 1) * WIDE] = piece[:, :WIDE]
            quad_ref[pl.ds(row + DD, DD), leg * WIDE : (leg + 1) * WIDE] = piece[:, WIDE:]
        return carry

    lax.fori_loop(0, HALF // 2, quad_step, 0, unroll=4)

    for pair in range(DD // 2):
        at = pair * 2 * WIDE
        block = dot(turned_ref[...], quad_ref[:, at : at + 2 * WIDE])
        rightward_ref[:, pair * WIDE : (pair + 1) * WIDE] = gather_pair(block[:WIDE]).astype(BF)
        sketched_ref[:, pair * WIDE : (pair + 1) * WIDE] = gather_pair(block[WIDE:]).astype(BF)
    down = dot_nt(quad_ref[...], gwide_ref[...])
    downward_ref[...] = from_rows(down, rows_ref).astype(BF)


def backward_kernel(
    below_ref, beside_ref, above_ref, behind_ref, cols_ref, gwide_ref, a_ref, tops_ref, first_ref, lwide_ref, corner_ref,
    top_out_ref, corner_out_ref, left_out_ref, dquad_ref, rows_ref, right_ref, left_ref, dsecond_ref,
):
    to_rows(below_ref[...], rows_ref, right_ref, 0)
    right_ref[:, WIDE:] = cols_ref[...]
    left_ref[:WIDE, :] = gwide_ref[...]
    spread(beside_ref[...], left_ref, WIDE)
    arrived = (above_ref[...].astype(F32) + behind_ref[...].astype(F32)).astype(BF)
    spread(arrived, left_ref, 2 * WIDE)

    def dquad_step(pair, carry):
        at = pl.multiple_of(pair * 2 * WIDE, 2 * WIDE)
        block = dot(right_ref[...], left_ref[:, pl.ds(at, 2 * WIDE)]).astype(BF)
        row = pl.multiple_of(pair * 2 * DD, 2 * DD)
        for one in range(HALF):
            piece = block[one * DD : (one + 1) * DD]
            dquad_ref[pl.ds(row, DD), one * WIDE : (one + 1) * WIDE] = piece[:, :WIDE]
            dquad_ref[pl.ds(row + DD, DD), one * WIDE : (one + 1) * WIDE] = piece[:, WIDE:]
        return carry

    lax.fori_loop(0, DD // 2, dquad_step, 0, unroll=2)
    a_turned = a_ref[...].T

    def dsecond_step(pair, carry):
        at = pl.multiple_of(pair * 2 * WIDE, 2 * WIDE)
        block = dot(a_turned, dquad_ref[:, pl.ds(at, 2 * WIDE)]).astype(BF)
        row = pl.multiple_of(pair * 2 * DD, 2 * DD)
        for leg in range(DD):
            piece = block[leg * DD : (leg + 1) * DD]
            dsecond_ref[pl.ds(row, DD), leg * WIDE : (leg + 1) * WIDE] = piece[:, :WIDE]
            dsecond_ref[pl.ds(row + DD, DD), leg * WIDE : (leg + 1) * WIDE] = piece[:, WIDE:]
        return carry

    lax.fori_loop(0, HALF // 2, dsecond_step, 0, unroll=4)

    first_turned = first_ref[...].T
    for pair in range(DD // 2):
        at = pair * 2 * WIDE
        block = dot(first_turned, dsecond_ref[:, at : at + 2 * WIDE])
        left_out_ref[:, pair * WIDE : (pair + 1) * WIDE] = gather_pair(block).astype(BF)
    dfirst = dot_nt(dsecond_ref[...], lwide_ref[...]).astype(BF)
    corner = corner_ref[...]
    nothing = jnp.zeros((CHI, CHI), BF)
    corner_two = jnp.concatenate(
        [jnp.concatenate([corner, nothing], axis=1), jnp.concatenate([nothing, corner], axis=1)], axis=0
    )
    dtop = dot(dfirst, corner_two)
    top_out_ref[...] = from_rows(dtop, rows_ref).astype(BF)
    dcorner = dot_tn(dfirst, tops_ref[...])
    corner_out_ref[...] = (dcorner[:CHI, :CHI] + pltpu.roll(dcorner[CHI:], CHI, 1)[:, :CHI]).astype(BF)


def split(value):
    high = value.astype(BF)
    return high, (value - high.astype(F32)).astype(BF)


def site_kernel(dquad_ref, second_ref, ket_ref, bra_ref, out_ref):
    grad = dot_nt(dquad_ref[...], second_ref[...])
    ket_map, bra_map = leg_maps()
    for phys in range(2):
        total = None
        for other_ref, leg_map in ((ket_ref, bra_map), (bra_ref, ket_map)):
            for part in split(grad * other_ref[phys].astype(F32)):
                half = dot_nt(leg_map, part)
                for piece in split(half):
                    term = dot_nt(piece, leg_map)
                    total = term if total is None else total + term
        out_ref[phys] = total


def shape(*dims, dtype=BF):
    return jax.ShapeDtypeStruct(dims, dtype)


def call(kernel, outs, scratch, flops, moved):
    return pl.pallas_call(
        kernel,
        out_shape=outs,
        scratch_shapes=scratch,
        compiler_params=pltpu.CompilerParams(vmem_limit_bytes=24 << 20),
        cost_estimate=pl.CostEstimate(flops=flops, bytes_accessed=moved, transcendentals=0),
    )


def from_behind(value, axis, by):
    length = lax.axis_size(axis)
    return lax.ppermute(value, axis, [(i, (i + by) % length) for i in range(length)])


def local(corner, top_edge, left_edge, site_tensor, sketch, grad_left, grad_top):
    own_corner = corner[0, 0]
    own_top = top_edge[0, 0]
    own_left = left_edge[0, 0]
    own_sketch = sketch[0, 0]
    own_gleft = grad_left[0, 0]
    own_gtop = grad_top[0, 0]
    site = site_tensor.reshape(2, DD, DD)
    corner_above, top_used = from_behind((own_corner, own_top), "row", 1)
    corner_used, left_used = from_behind((corner_above, own_left), "col", 1)
    rows = pltpu.VMEM((ORDER, WIDE), F32)
    a_mat, ket, bra, cols, turned, gwide = call(
        prepare_kernel,
        (
            shape(256, 256), shape(2, 256, 256), shape(2, 256, 256), shape(512, 256), shape(256, 512), shape(128, 2048),
        ),
        [rows],
        10**7, 2 * 10**6,
    )(site, own_sketch, own_gtop, own_gleft)
    sketched, downward, rightward, tops, first, lwide, second = call(
        forward_kernel,
        (
            shape(CHI, ORDER), shape(CHI, ORDER), shape(CHI, ORDER),
            shape(512, WIDE), shape(512, WIDE), shape(WIDE, 2048), shape(256, 4096),
        ),
        [rows, pltpu.VMEM((512, 2048), BF)],
        2 * 10**9, 4 * 10**6,
    )(corner_used, top_used, left_used, a_mat, turned, gwide)
    sketch_below = from_behind(sketched, "row", -1)
    sketch_beside = from_behind(sketched, "col", -1)
    from_above = from_behind(downward, "row", 1)
    from_left = from_behind(rightward, "col", 1)
    grad_topped, grad_cornered, grad_lefted, dquad = call(
        backward_kernel,
        (shape(CHI, ORDER), shape(CHI, CHI), shape(CHI, ORDER), shape(256, 4096)),
        [rows, pltpu.VMEM((512, 384), BF), pltpu.VMEM((384, 2048), BF), pltpu.VMEM((512, 2048), BF)],
        3 * 10**9, 6 * 10**6,
    )(sketch_below, sketch_beside, from_above, from_left, cols, gwide, a_mat, tops, first, lwide, corner_used)
    top_result, corner_mid = from_behind((grad_topped, grad_cornered), "row", -1)
    left_result, corner_result = from_behind((grad_lefted, corner_mid), "col", -1)
    site_result = call(
        site_kernel, shape(2, DD, DD, dtype=F32), [], 10**9, 5 * 10**6
    )(dquad, second, ket, bra)
    return (
        corner_result[None, None],
        top_result[None, None],
        left_result[None, None],
        site_result.reshape(site_tensor.shape),
    )


def solution(mesh):
    flat = P("row", "col", None, None)
    deep = P("row", "col", None, None, None, None, None)
    return jax.shard_map(
        local,
        mesh=mesh,
        in_specs=(flat, flat, flat, deep, flat, flat, flat),
        out_specs=(flat, flat, flat, deep),
        check_vma=False,
    )
```

time: 202 us -> 57.5 us (0.28); the launches traced: 198 us -> 57.3 us
  matrix products: 128 us -> 0 us
  local copies, waits for them, and re-layouts: 33.1 us -> 6.23 us
  Pallas kernels: 0 us -> 14.2 us
  waiting for transfers between devices: 8.38 us -> 13.5 us
  starting transfers between devices: 25.4 us -> 22.7 us
    dot_general x27 -> x0, matrix products: 127 us -> none  [the longest x2 46.5 us: local(): jnp.einsum('pbmevst,szmvxt->pebxz', ket_layer, grad_quad, preferred_eleme...]
    pallas_call x0 -> x4, Pallas kernels: none -> 14.2 us  [the longest x1 5.49 us: local(): call(backward_kernel, (shape(CHI, ORDER), shape(CHI, CHI), shape(CHI, ORD...]
    reshape x9 -> x2, local copies, waits for them, and re-layouts: 13.4 us -> 1.61 us  [the longest x1 0.85 us: local(): site = site_tensor.reshape(2, DD, DD)]
    squeeze x4 -> x0, local copies, waits for them, and re-layouts: 6.69 us -> none  [local(): tensor_site = site_tensor[0, 0]]
    ppermute x12, waiting for transfers between devices: 8.38 us -> 13.5 us  [from_behind(): lax.ppermute(value, axis, [(i, (i + by) % length) for i in range(length)])]
    convert_element_type x6 -> x0, local copies, waits for them, and re-layouts: 4.06 us -> none  [the longest x2 2.01 us: local(): grad_second = jnp.einsum('pbmevst,pcavs->abmcet', grad_ket, tensor_site,...]
    ppermute x12, starting transfers between devices: 25.4 us -> 22.7 us  [from_behind(): lax.ppermute(value, axis, [(i, (i + by) % length) for i in range(length)])]
    unnamed x60 -> x9, local copies, waits for them, and re-layouts: 4.12 us -> 4.62 us
  transfers between devices with their start and end apart: 12 -> 12, of which waited for: 3 -> 4; matrix products, arithmetic and copies ran while one was open for 18% -> 3% of each run, Pallas kernels for 0% -> 7%
where the time goes in v1:
time: 57.5 us; the launch traced here: 57.3 us
  starting transfers between devices  22.7 us (39%)
  Pallas kernels  14.2 us (25%)
  waiting for transfers between devices  13.5 us (23%)
  local copies, waits for them, and re-layouts  6.23 us (11%)
  between operations  0.72 us (1%)
    ppermute x12, starting transfers between devices, from_behind(): lax.ppermute(value, axis, [(i, (i + by) % length) for i in range(length)])  22.7 us
    ppermute x12, waiting for transfers between devices, from_behind(): lax.ppermute(value, axis, [(i, (i + by) % length) for i in range(length)])  13.5 us
    pallas_call x1, Pallas kernels, local(): call(backward_kernel, (shape(CHI, ORDER), shape(CHI, CHI), shape(CHI, ORD...  5.49 us
    pallas_call x1, Pallas kernels, local(): call(forward_kernel, (shape(CHI, ORDER), shape(CHI, ORDER), shape(CHI, OR...  4.89 us
    unnamed x9, local copies, waits for them, and re-layouts  4.62 us
    pallas_call x1, Pallas kernels, local(): call(site_kernel, shape(2, DD, DD, dtype=F32), [], 10 ** 9, 5 * 10 ** 6)  2.54 us
    pallas_call x1, Pallas kernels, local(): call(prepare_kernel, (shape(256, 256), shape(2, 256, 256), shape(2, 256,...  1.27 us
  transfers between devices with their start and end apart: 12, of which 4 were waited for; matrix products, arithmetic and copies ran while one was open for 3% of the time, Pallas kernels for 7%

profile of v1, /device:TPU:1, one launch (start us, length us, event | category | flops | bytes accessed | tf_op | source)
XLA Modules:
  0.0 57.3 jit_solution(8936824032265415293)
XLA Ops:
  0.6 2.1 %collective-permute-start.2 = (bf16[64,1024]{1,0:T(8,128)(2,1)}, bf16[64,1024]{1,0:T(8,128)(2,1)S(1)}, u32[]{:S(2)}, u32[]{:S(2)}) collective-permute-start(bf16[64,1024]{1,0:T(8,128)(2,1)} %bitcast.15), channel_id=1, source_target_pairs={{0,16},{16,32},{32,48},{48,64},{64,80},{80,96},{96,112},{112,128},... | collective-permute-start | bytes 393224 | tf_op jit(solution)/shard_map/ppermute | solution.py:241
  2.7 3.3 %collective-permute-start.3 = (bf16[64,1024]{1,0:T(8,128)(2,1)}, bf16[64,1024]{1,0:T(8,128)(2,1)S(1)}, u32[]{:S(2)}, u32[]{:S(2)}) collective-permute-start(bf16[64,1024]{1,0:T(8,128)(2,1)} %bitcast.16), channel_id=1, source_target_pairs={{0,1},{1,2},{2,3},{3,4},{4,5},{5,6},{6,7},{7,8},{8,9},{9,10},{10,1... | collective-permute-start | bytes 393224 | tf_op jit(solution)/shard_map/ppermute | solution.py:241
  6.0 1.3 %collective-permute-start = (bf16[64,64]{1,0:T(8,128)(2,1)}, bf16[64,64]{1,0:T(8,128)(2,1)S(1)}, u32[]{:S(2)}, u32[]{:S(2)}) collective-permute-start(bf16[64,64]{1,0:T(8,128)(2,1)} %bitcast.17), channel_id=1, source_target_pairs={{0,16},{16,32},{32,48},{48,64},{64,80},{80,96},{96,112},{112,128},... | collective-permute-start | bytes 24584 | tf_op jit(solution)/shard_map/ppermute | solution.py:241
  7.3 5.0 %collective-permute-done = bf16[64,64]{1,0:T(8,128)(2,1)S(1)} collective-permute-done((bf16[64,64]{1,0:T(8,128)(2,1)}, bf16[64,64]{1,0:T(8,128)(2,1)S(1)}, u32[]{:S(2)}, u32[]{:S(2)}) %collective-permute-start) | collective-permute-done | bytes 8224 | tf_op jit(solution)/shard_map/ppermute | solution.py:241
  12.3 3.2 %collective-permute-start.1 = (bf16[64,64]{1,0:T(8,128)(2,1)S(1)}, bf16[64,64]{1,0:T(8,128)(2,1)S(1)}, u32[]{:S(2)}, u32[]{:S(2)}) collective-permute-start(bf16[64,64]{1,0:T(8,128)(2,1)S(1)} %collective-permute-done), channel_id=1, source_target_pairs={{0,1},{1,2},{2,3},{3,4},{4,5},{5,6},{6,7},{7,8},{8,9},{9,10},{10,1... | collective-permute-start | bytes 24584 | tf_op jit(solution)/shard_map/ppermute | solution.py:241
  15.5 0.8 %reshape.14.site_ref = bf16[2,16,16]{2,1,0:T(8,128)(2,1)S(1)} reshape(bf16[1,1,2,4,4,4,4]{6,5,4,3,2,1,0:T(4,128)(2,1)} %param.10) | data formatting | bytes 2048 | tf_op jit(solution)/shard_map/reshape | solution.py:251
  16.3 0.0 copy-start
  16.3 0.9 %copy-done = bf16[1,1,64,1024]{3,2,1,0:T(8,128)(2,1)S(1)} copy-done((bf16[1,1,64,1024]{3,2,1,0:T(8,128)(2,1)S(1)}, bf16[1,1,64,1024]{3,2,1,0:T(8,128)(2,1)}, u32[]{:S(2)}) %copy-start) | copy-done | bytes 131096
  17.2 0.9 %copy-done.1 = bf16[1,1,64,1024]{3,2,1,0:T(8,128)(2,1)S(1)} copy-done((bf16[1,1,64,1024]{3,2,1,0:T(8,128)(2,1)S(1)}, bf16[1,1,64,1024]{3,2,1,0:T(8,128)(2,1)}, u32[]{:S(2)}) %copy-start.1) | copy-done | bytes 131096
  18.1 0.9 %copy-done.2 = bf16[1,1,64,1024]{3,2,1,0:T(8,128)(2,1)S(1)} copy-done((bf16[1,1,64,1024]{3,2,1,0:T(8,128)(2,1)S(1)}, bf16[1,1,64,1024]{3,2,1,0:T(8,128)(2,1)}, u32[]{:S(2)}) %copy-start.2) | copy-done | bytes 131096
  19.1 1.3 %shard_map.102 = (bf16[256,256]{1,0:T(8,128)(2,1)S(1)}, bf16[2,256,256]{2,1,0:T(8,128)(2,1)S(1)}, bf16[2,256,256]{2,1,0:T(8,128)(2,1)S(1)}, bf16[512,256]{1,0:T(...) custom-call(bf16[2,16,16]{2,1,0:T(8,128)(2,1)S(1)} %reshape.14.site_ref, ...), custom_call_target="tpu_custom_call" | custom-call | flops 10000000 | bytes 2000000 | tf_op jit(solution)/shard_map/pallas_call | solution.py:255
  20.3 0.0 collective-permute-done.1.corner_ref
  20.3 0.0 collective-permute-done.3.left_ref
  20.4 4.9 %shard_map.103 = (bf16[64,1024]{1,0:T(8,128)(2,1)S(1)}, bf16[64,1024]{1,0:T(8,128)(2,1)S(1)}, bf16[64,1024]{1,0:T(8,128)(2,1)S(1)}, bf16[512,128]{1,0:T(8,128)(2...) custom-call(bf16[64,64]{1,0:T(8,128)(2,1)S(1)} %collective-permute-done.1.corner, ...), custom_call_target="tpu_custom_call" | custom-call | flops 2000000000 | bytes 4000000 | tf_op jit(solution)/shard_map/pallas_call | solution.py:263
  25.3 0.1 collective-permute-start.6
  25.3 0.1 collective-permute-start.7
  25.4 0.5 collective-permute-start.5
  25.9 3.5 %collective-permute-start.4 = (bf16[64,1024]{1,0:T(8,128)(2,1)S(1)}, bf16[64,1024]{1,0:T(8,128)(2,1)S(1)}, u32[]{:S(2)}, u32[]{:S(2)}) collective-permute-start(bf16[64,1024]{1,0:T(8,128)(2,1)S(1)} %get-tuple-element.24), channel_id=1, source_target_pairs={{0,240},{16,0},{32,16},{48,32},{64,48},{80,64},{96,80},{112,96},{1... | collective-permute-start | bytes 393224 | tf_op jit(solution)/shard_map/ppermute | solution.py:241
  29.4 3.5 %collective-permute-done.6.above_ref = bf16[64,1024]{1,0:T(8,128)(2,1)S(1)} collective-permute-done((bf16[64,1024]{1,0:T(8,128)(2,1)S(1)}, bf16[64,1024]{1,0:T(8,128)(2,1)S(1)}, u32[]{:S(2)}, u32[]{:S(2)}) %collective-permute-start.6) | collective-permute-done | bytes 131104 | tf_op jit(solution)/shard_map/ppermute | solution.py:241
  32.9 0.0 collective-permute-done.7.behind_ref
  32.9 2.4 %collective-permute-done.5.beside_ref = bf16[64,1024]{1,0:T(8,128)(2,1)S(1)} collective-permute-done((bf16[64,1024]{1,0:T(8,128)(2,1)S(1)}, bf16[64,1024]{1,0:T(8,128)(2,1)S(1)}, u32[]{:S(2)}, u32[]{:S(2)}) %collective-permute-start.5) | collective-permute-done | bytes 131104 | tf_op jit(solution)/shard_map/ppermute | solution.py:241
  35.3 0.0 collective-permute-done.4.below_ref
  35.3 5.5 %shard_map.104 = (bf16[64,1024]{1,0:T(8,128)(2,1)S(1)}, bf16[64,64]{1,0:T(8,128)(2,1)S(1)}, bf16[64,1024]{1,0:T(8,128)(2,1)S(1)}, bf16[256,4096]{1,0:T(8,128)(2,1)S(1)}) custom-call(bf16[64,1024]{1,0:T(8,128)(2,1)S(1)} %collective-permute-done.4.below_ref, bf16[64,1024]{1,0:T(8,128)(2,1)S(1)} %collective-permute-done.5.beside_ref, ...), custom_call_target="tpu_custom_call" | custom-call | flops 3000000000 | bytes 6000000 | tf_op jit(solution)/shard_map/pallas_call | solution.py:276
  40.8 1.3 %collective-permute-start.10 = (bf16[64,1024]{1,0:T(8,128)(2,1)S(1)}, bf16[64,1024]{1,0:T(8,128)(2,1)S(1)}, u32[]{:S(2)}, u32[]{:S(2)}) collective-permute-start(bf16[64,1024]{1,0:T(8,128)(2,1)S(1)} %get-tuple-element.32), channel_id=1, source_target_pairs={{0,240},{16,0},{32,16},{48,32},{64,48},{80,64},{96,80},{112,96},{1... | collective-permute-start | bytes 393224 | tf_op jit(solution)/shard_map/ppermute | solution.py:241
  42.1 5.0 %collective-permute-start.11 = (bf16[64,1024]{1,0:T(8,128)(2,1)S(1)}, bf16[64,1024]{1,0:T(8,128)(2,1)S(1)}, u32[]{:S(2)}, u32[]{:S(2)}) collective-permute-start(bf16[64,1024]{1,0:T(8,128)(2,1)S(1)} %get-tuple-element.33), channel_id=1, source_target_pairs={{0,15},{1,0},{2,1},{3,2},{4,3},{5,4},{6,5},{7,6},{8,7},{9,8},{10,9... | collective-permute-start | bytes 393224 | tf_op jit(solution)/shard_map/ppermute | solution.py:241
  47.1 2.6 %collective-permute-done.8 = bf16[64,64]{1,0:T(8,128)(2,1)S(1)} collective-permute-done((bf16[64,64]{1,0:T(8,128)(2,1)S(1)}, bf16[64,64]{1,0:T(8,128)(2,1)S(1)}, u32[]{:S(2)}, u32[]{:S(2)}) %collective-permute-start.8) | collective-permute-done | bytes 8224 | tf_op jit(solution)/shard_map/ppermute | solution.py:241
  49.7 2.4 %collective-permute-start.9 = (bf16[64,64]{1,0:T(8,128)(2,1)S(1)}, bf16[64,64]{1,0:T(8,128)(2,1)S(1)}, u32[]{:S(2)}, u32[]{:S(2)}) collective-permute-start(bf16[64,64]{1,0:T(8,128)(2,1)S(1)} %collective-permute-done.8), channel_id=1, source_target_pairs={{0,15},{1,0},{2,1},{3,2},{4,3},{5,4},{6,5},{7,6},{8,7},{9,8},{10,9... | collective-permute-start | bytes 24584 | tf_op jit(solution)/shard_map/ppermute | solution.py:241
  52.1 2.5 %shard_map.105 = f32[2,16,16]{2,1,0:T(8,128)S(1)} custom-call(bf16[256,4096]{1,0:T(8,128)(2,1)S(1)} %get-tuple-element.34.dquad_ref, bf16[256,4096]{1,0:T(8,128)(2,1)S(1)} %get-tuple-element.35.second_ref, bf16[2,256,256]{2,1,0:T(8,128)(2,1)S(1)} %get-tuple-element.36.ket_ref, bf16[2,256,256]{2,1,0:T(8,128)(2,1)S(1)} %get-tuple-element.37.bra_ref), custom_call_target="tpu_custom_call" | custom-call | flops 1000000000 | bytes 5000000 | tf_op jit(solution)/shard_map/pallas_call | solution.py:284
  54.6 0.8 %reshape.15 = f32[1,1,2,4,4,4,4]{6,5,4,3,2,1,0:T(4,128)} reshape(f32[2,16,16]{2,1,0:T(8,128)S(1)} %shard_map.105) | data formatting | bytes 4096 | tf_op jit(solution)/shard_map/reshape | solution.py:291
  55.4 0.6 %copy.14 = bf16[1,1,64,64]{3,2,1,0:T(8,128)(2,1)} copy(bf16[1,1,64,64]{3,2,1,0:T(8,128)(2,1)S(1)} %bitcast.14) | data formatting | bytes 16384
  56.0 0.7 %copy.15 = bf16[1,1,64,1024]{3,2,1,0:T(8,128)(2,1)} copy(bf16[1,1,64,1024]{3,2,1,0:T(8,128)(2,1)S(1)} %bitcast.12) | data formatting | bytes 262144
  56.7 0.7 %copy.16 = bf16[1,1,64,1024]{3,2,1,0:T(8,128)(2,1)} copy(bf16[1,1,64,1024]{3,2,1,0:T(8,128)(2,1)S(1)} %bitcast.13) | data formatting | bytes 262144
  (7 shorter events, 0.0 us)
Async XLA Ops:
  0.6 19.7 %collective-permute-start.2 = (bf16[64,1024]{1,0:T(8,128)(2,1)}, bf16[64,1024]{1,0:T(8,128)(2,1)S(1)}, u32[]{:S(2)}, u32[]{:S(2)}) collective-permute-start(bf16[64,1024]{1,0:T(8,128)(2,1)} %bitcast.15), channel_id=1, source_target_pairs={{0,16},{16,32},{32,48},{48,64},{64,80},{80,96},{96,112},{112,128},... | collective-permute-start | bytes 393224 | tf_op jit(solution)/shard_map/ppermute | solution.py:241
  2.7 17.6 %collective-permute-start.3 = (bf16[64,1024]{1,0:T(8,128)(2,1)}, bf16[64,1024]{1,0:T(8,128)(2,1)S(1)}, u32[]{:S(2)}, u32[]{:S(2)}) collective-permute-start(bf16[64,1024]{1,0:T(8,128)(2,1)} %bitcast.16), channel_id=1, source_target_pairs={{0,1},{1,2},{2,3},{3,4},{4,5},{5,6},{6,7},{7,8},{8,9},{9,10},{10,1... | collective-permute-start | bytes 393224 | tf_op jit(solution)/shard_map/ppermute | solution.py:241
  6.0 6.3 %collective-permute-start = (bf16[64,64]{1,0:T(8,128)(2,1)}, bf16[64,64]{1,0:T(8,128)(2,1)S(1)}, u32[]{:S(2)}, u32[]{:S(2)}) collective-permute-start(bf16[64,64]{1,0:T(8,128)(2,1)} %bitcast.17), channel_id=1, source_target_pairs={{0,16},{16,32},{32,48},{48,64},{64,80},{80,96},{96,112},{112,128},... | collective-permute-start | bytes 24584 | tf_op jit(solution)/shard_map/ppermute | solution.py:241
  12.3 8.0 %collective-permute-start.1 = (bf16[64,64]{1,0:T(8,128)(2,1)S(1)}, bf16[64,64]{1,0:T(8,128)(2,1)S(1)}, u32[]{:S(2)}, u32[]{:S(2)}) collective-permute-start(bf16[64,64]{1,0:T(8,128)(2,1)S(1)} %collective-permute-done), channel_id=1, source_target_pairs={{0,1},{1,2},{2,3},{3,4},{4,5},{5,6},{6,7},{7,8},{8,9},{9,10},{10,1... | collective-permute-start | bytes 24584 | tf_op jit(solution)/shard_map/ppermute | solution.py:241
  16.3 0.9 %copy-start = (bf16[1,1,64,1024]{3,2,1,0:T(8,128)(2,1)S(1)}, bf16[1,1,64,1024]{3,2,1,0:T(8,128)(2,1)}, u32[]{:S(2)}) copy-start(bf16[1,1,64,1024]{3,2,1,0:T(8,128)(2,1)} %param.11) | copy-start | bytes 393220
  17.2 0.9 %copy-start.1 = (bf16[1,1,64,1024]{3,2,1,0:T(8,128)(2,1)S(1)}, bf16[1,1,64,1024]{3,2,1,0:T(8,128)(2,1)}, u32[]{:S(2)}) copy-start(bf16[1,1,64,1024]{3,2,1,0:T(8,128)(2,1)} %param.13) | copy-start | bytes 393220
  18.1 0.9 %copy-start.2 = (bf16[1,1,64,1024]{3,2,1,0:T(8,128)(2,1)S(1)}, bf16[1,1,64,1024]{3,2,1,0:T(8,128)(2,1)}, u32[]{:S(2)}) copy-start(bf16[1,1,64,1024]{3,2,1,0:T(8,128)(2,1)} %param.12) | copy-start | bytes 393220
  25.3 7.7 %collective-permute-start.6 = (bf16[64,1024]{1,0:T(8,128)(2,1)S(1)}, bf16[64,1024]{1,0:T(8,128)(2,1)S(1)}, u32[]{:S(2)}, u32[]{:S(2)}) collective-permute-start(bf16[64,1024]{1,0:T(8,128)(2,1)S(1)} %get-tuple-element.25), channel_id=1, source_target_pairs={{0,16},{16,32},{32,48},{48,64},{64,80},{80,96},{96,112},{112,128},... | collective-permute-start | bytes 393224 | tf_op jit(solution)/shard_map/ppermute | solution.py:241
  25.3 7.6 %collective-permute-start.7 = (bf16[64,1024]{1,0:T(8,128)(2,1)S(1)}, bf16[64,1024]{1,0:T(8,128)(2,1)S(1)}, u32[]{:S(2)}, u32[]{:S(2)}) collective-permute-start(bf16[64,1024]{1,0:T(8,128)(2,1)S(1)} %get-tuple-element.26), channel_id=1, source_target_pairs={{0,1},{1,2},{2,3},{3,4},{4,5},{5,6},{6,7},{7,8},{8,9},{9,10},{10,1... | collective-permute-start | bytes 393224 | tf_op jit(solution)/shard_map/ppermute | solution.py:241
  25.4 9.9 %collective-permute-start.5 = (bf16[64,1024]{1,0:T(8,128)(2,1)S(1)}, bf16[64,1024]{1,0:T(8,128)(2,1)S(1)}, u32[]{:S(2)}, u32[]{:S(2)}) collective-permute-start(bf16[64,1024]{1,0:T(8,128)(2,1)S(1)} %get-tuple-element.24), channel_id=1, source_target_pairs={{0,15},{1,0},{2,1},{3,2},{4,3},{5,4},{6,5},{7,6},{8,7},{9,8},{10,9... | collective-permute-start | bytes 393224 | tf_op jit(solution)/shard_map/ppermute | solution.py:241
  25.9 9.4 %collective-permute-start.4 = (bf16[64,1024]{1,0:T(8,128)(2,1)S(1)}, bf16[64,1024]{1,0:T(8,128)(2,1)S(1)}, u32[]{:S(2)}, u32[]{:S(2)}) collective-permute-start(bf16[64,1024]{1,0:T(8,128)(2,1)S(1)} %get-tuple-element.24), channel_id=1, source_target_pairs={{0,240},{16,0},{32,16},{48,32},{64,48},{80,64},{96,80},{112,96},{1... | collective-permute-start | bytes 393224 | tf_op jit(solution)/shard_map/ppermute | solution.py:241
  40.8 14.6 %collective-permute-start.10 = (bf16[64,1024]{1,0:T(8,128)(2,1)S(1)}, bf16[64,1024]{1,0:T(8,128)(2,1)S(1)}, u32[]{:S(2)}, u32[]{:S(2)}) collective-permute-start(bf16[64,1024]{1,0:T(8,128)(2,1)S(1)} %get-tuple-element.32), channel_id=1, source_target_pairs={{0,240},{16,0},{32,16},{48,32},{64,48},{80,64},{96,80},{112,96},{1... | collective-permute-start | bytes 393224 | tf_op jit(solution)/shard_map/ppermute | solution.py:241
  42.1 13.3 %collective-permute-start.11 = (bf16[64,1024]{1,0:T(8,128)(2,1)S(1)}, bf16[64,1024]{1,0:T(8,128)(2,1)S(1)}, u32[]{:S(2)}, u32[]{:S(2)}) collective-permute-start(bf16[64,1024]{1,0:T(8,128)(2,1)S(1)} %get-tuple-element.33), channel_id=1, source_target_pairs={{0,15},{1,0},{2,1},{3,2},{4,3},{5,4},{6,5},{7,6},{8,7},{9,8},{10,9... | collective-permute-start | bytes 393224 | tf_op jit(solution)/shard_map/ppermute | solution.py:241
  47.1 2.6 %collective-permute-start.8 = (bf16[64,64]{1,0:T(8,128)(2,1)S(1)}, bf16[64,64]{1,0:T(8,128)(2,1)S(1)}, u32[]{:S(2)}, u32[]{:S(2)}) collective-permute-start(bf16[64,64]{1,0:T(8,128)(2,1)S(1)} %get-tuple-element.31), channel_id=1, source_target_pairs={{0,240},{16,0},{32,16},{48,32},{64,48},{80,64},{96,80},{112,96},{1... | collective-permute-start | bytes 24584 | tf_op jit(solution)/shard_map/ppermute | solution.py:241
  49.7 5.7 %collective-permute-start.9 = (bf16[64,64]{1,0:T(8,128)(2,1)S(1)}, bf16[64,64]{1,0:T(8,128)(2,1)S(1)}, u32[]{:S(2)}, u32[]{:S(2)}) collective-permute-start(bf16[64,64]{1,0:T(8,128)(2,1)S(1)} %collective-permute-done.8), channel_id=1, source_target_pairs={{0,15},{1,0},{2,1},{3,2},{4,3},{5,4},{6,5},{7,6},{8,7},{9,8},{10,9... | collective-permute-start | bytes 24584 | tf_op jit(solution)/shard_map/ppermute | solution.py:241

commit v2 on v1

--- a/solution.py
+++ b/solution.py
@@ -1,11 +1,10 @@
-import functools
-
 import jax
 import jax.numpy as jnp
 from jax import lax
 from jax.experimental import pallas as pl
 from jax.experimental.pallas import tpu as pltpu
 from jax.sharding import PartitionSpec as P
+
 
 BF = jnp.bfloat16
 F32 = jnp.float32
@@ -14,6 +13,7 @@
 ORDER = DD * CHI
 HALF = CHI // 2
 WIDE = 2 * CHI
+PREP = 20 << 20
 
 
 def dot(lhs, rhs):
@@ -87,7 +87,19 @@
     return ket_c.astype(BF), bra_c.astype(BF)
 
 
-def prepare_kernel(site_ref, sketch_ref, gtop_ref, gleft_ref, a_ref, ket_ref, bra_ref, cols_ref, turned_ref, gwide_ref, rows_ref):
+def prepare_kernel(
+    site_ref, sketch_hbm, gtop_hbm, gleft_hbm,
+    a_ref, ket_ref, bra_ref, cols_ref, turned_ref, gwide_ref,
+    rows_ref, sketch_ref, gtop_ref, gleft_ref, sems,
+):
+    copies = [
+        pltpu.make_async_copy(source, target, sems.at[at])
+        for at, (source, target) in enumerate(
+            ((gtop_hbm, gtop_ref), (sketch_hbm, sketch_ref), (gleft_hbm, gleft_ref))
+        )
+    ]
+    for copy in copies:
+        copy.start()
     ket_map, bra_map = leg_maps()
     total = None
     for phys in range(2):
@@ -98,23 +110,29 @@
         bra_ref[phys] = bra.astype(BF)
         total = ket * bra if total is None else total + ket * bra
     a_ref[...] = total.astype(BF)
+    copies[0].wait()
     to_rows(gtop_ref[...], rows_ref, cols_ref, 0)
+    copies[1].wait()
     to_rows(sketch_ref[...], rows_ref, cols_ref, WIDE)
     turned_ref[...] = cols_ref[...].T
+    copies[2].wait()
     spread(gleft_ref[...], gwide_ref, 0)
 
 
+def corner_pair(corner):
+    nothing = jnp.zeros((CHI, CHI), BF)
+    return jnp.concatenate(
+        [jnp.concatenate([corner, nothing], axis=1), jnp.concatenate([nothing, corner], axis=1)], axis=0
+    )
+
+
 def forward_kernel(
-    corner_ref, top_ref, left_ref, a_ref, turned_ref, gwide_ref,
-    sketched_ref, downward_ref, rightward_ref, tops_ref, first_ref, lwide_ref, second_ref, rows_ref, quad_ref,
+    corner_ref, top_ref, left_ref, a_ref, turned_ref,
+    sketched_ref, rightward_ref, tops_ref, first_ref, lwide_ref, second_ref, quad_ref,
+    rows_ref,
 ):
     to_rows(top_ref[...], rows_ref, tops_ref, 0)
-    corner = corner_ref[...]
-    nothing = jnp.zeros((CHI, CHI), BF)
-    corner_two = jnp.concatenate(
-        [jnp.concatenate([corner, nothing], axis=1), jnp.concatenate([nothing, corner], axis=1)], axis=0
-    )
-    first_ref[...] = dot_nt(tops_ref[...], corner_two).astype(BF)
+    first_ref[...] = dot_nt(tops_ref[...], corner_pair(corner_ref[...])).astype(BF)
     spread(left_ref[...], lwide_ref, 0)
 
     def second_step(pair, carry):
@@ -146,24 +164,39 @@
         block = dot(turned_ref[...], quad_ref[:, at : at + 2 * WIDE])
         rightward_ref[:, pair * WIDE : (pair + 1) * WIDE] = gather_pair(block[:WIDE]).astype(BF)
         sketched_ref[:, pair * WIDE : (pair + 1) * WIDE] = gather_pair(block[WIDE:]).astype(BF)
+
+
+def downward_kernel(quad_ref, gwide_ref, downward_ref, rows_ref):
     down = dot_nt(quad_ref[...], gwide_ref[...])
     downward_ref[...] = from_rows(down, rows_ref).astype(BF)
 
 
-def backward_kernel(
-    below_ref, beside_ref, above_ref, behind_ref, cols_ref, gwide_ref, a_ref, tops_ref, first_ref, lwide_ref, corner_ref,
-    top_out_ref, corner_out_ref, left_out_ref, dquad_ref, rows_ref, right_ref, left_ref, dsecond_ref,
-):
+def partial_kernel(below_ref, beside_ref, cols_ref, gwide_ref, part_ref, rows_ref, right_ref, left_ref):
     to_rows(below_ref[...], rows_ref, right_ref, 0)
-    right_ref[:, WIDE:] = cols_ref[...]
+    right_ref[:, WIDE:] = cols_ref[:, :WIDE]
     left_ref[:WIDE, :] = gwide_ref[...]
     spread(beside_ref[...], left_ref, WIDE)
+
+    def step(pair, carry):
+        at = pl.multiple_of(pair * 2 * WIDE, 2 * WIDE)
+        part_ref[:, pl.ds(at, 2 * WIDE)] = dot(right_ref[...], left_ref[:, pl.ds(at, 2 * WIDE)])
+        return carry
+
+    lax.fori_loop(0, DD // 2, step, 0, unroll=2)
+
+
+def backward_kernel(
+    above_ref, behind_ref, part_ref, cols_ref, a_ref, first_ref,
+    left_out_ref, dquad_ref, dsecond_ref,
+    left_ref,
+):
     arrived = (above_ref[...].astype(F32) + behind_ref[...].astype(F32)).astype(BF)
-    spread(arrived, left_ref, 2 * WIDE)
+    spread(arrived, left_ref, 0)
 
     def dquad_step(pair, carry):
         at = pl.multiple_of(pair * 2 * WIDE, 2 * WIDE)
-        block = dot(right_ref[...], left_ref[:, pl.ds(at, 2 * WIDE)]).astype(BF)
+        block = dot(cols_ref[:, WIDE:], left_ref[:, pl.ds(at, 2 * WIDE)])
+        block = (block + part_ref[:, pl.ds(at, 2 * WIDE)]).astype(BF)
         row = pl.multiple_of(pair * 2 * DD, 2 * DD)
         for one in range(HALF):
             piece = block[one * DD : (one + 1) * DD]
@@ -191,13 +224,11 @@
         at = pair * 2 * WIDE
         block = dot(first_turned, dsecond_ref[:, at : at + 2 * WIDE])
         left_out_ref[:, pair * WIDE : (pair + 1) * WIDE] = gather_pair(block).astype(BF)
+
+
+def edges_kernel(dsecond_ref, lwide_ref, tops_ref, corner_ref, top_out_ref, corner_out_ref, rows_ref):
     dfirst = dot_nt(dsecond_ref[...], lwide_ref[...]).astype(BF)
-    corner = corner_ref[...]
-    nothing = jnp.zeros((CHI, CHI), BF)
-    corner_two = jnp.concatenate(
-        [jnp.concatenate([corner, nothing], axis=1), jnp.concatenate([nothing, corner], axis=1)], axis=0
-    )
-    dtop = dot(dfirst, corner_two)
+    dtop = dot(dfirst, corner_pair(corner_ref[...]))
     top_out_ref[...] = from_rows(dtop, rows_ref).astype(BF)
     dcorner = dot_tn(dfirst, tops_ref[...])
     corner_out_ref[...] = (dcorner[:CHI, :CHI] + pltpu.roll(dcorner[CHI:], CHI, 1)[:, :CHI]).astype(BF)
@@ -222,68 +253,105 @@
         out_ref[phys] = total
 
 
+def finish_kernel(corner_ref, top_ref, left_ref, corner_hbm, top_hbm, left_hbm, sems):
+    copies = [
+        pltpu.make_async_copy(source, target, sems.at[at])
+        for at, (source, target) in enumerate(
+            ((left_ref, left_hbm), (top_ref, top_hbm), (corner_ref, corner_hbm))
+        )
+    ]
+    for copy in copies:
+        copy.start()
+    for copy in copies:
+        copy.wait()
+
+
 def shape(*dims, dtype=BF):
     return jax.ShapeDtypeStruct(dims, dtype)
 
 
-def call(kernel, outs, scratch, flops, moved):
+def call(kernel, outs, scratch, flops, moved, specs=None, out_specs=None, room=20 << 20):
+    extra = {} if specs is None else {"in_specs": specs}
+    if out_specs is not None:
+        extra["out_specs"] = out_specs
     return pl.pallas_call(
         kernel,
         out_shape=outs,
+        **extra,
         scratch_shapes=scratch,
-        compiler_params=pltpu.CompilerParams(vmem_limit_bytes=24 << 20),
+        compiler_params=pltpu.CompilerParams(vmem_limit_bytes=room),
         cost_estimate=pl.CostEstimate(flops=flops, bytes_accessed=moved, transcendentals=0),
     )
 
 
-def from_behind(value, axis, by):
-    length = lax.axis_size(axis)
-    return lax.ppermute(value, axis, [(i, (i + by) % length) for i in range(length)])
-
-
-def local(corner, top_edge, left_edge, site_tensor, sketch, grad_left, grad_top):
-    own_corner = corner[0, 0]
-    own_top = top_edge[0, 0]
-    own_left = left_edge[0, 0]
-    own_sketch = sketch[0, 0]
-    own_gleft = grad_left[0, 0]
-    own_gtop = grad_top[0, 0]
+def from_behind(value, down, right):
+    rows, columns = lax.axis_size("row"), lax.axis_size("col")
+    pairs = [
+        (i * columns + j, (i + down) % rows * columns + (j + right) % columns)
+        for i in range(rows)
+        for j in range(columns)
+    ]
+    return lax.ppermute(value, ("row", "col"), pairs)
+
+
+def step(corner, top_edge, left_edge, site_tensor, sketch, grad_left, grad_top):
     site = site_tensor.reshape(2, DD, DD)
-    corner_above, top_used = from_behind((own_corner, own_top), "row", 1)
-    corner_used, left_used = from_behind((corner_above, own_left), "col", 1)
+    left_used = from_behind(left_edge[0, 0], 0, 1)
+    top_used = from_behind(top_edge[0, 0], 1, 0)
+    corner_used = from_behind(corner[0, 0], 1, 1)
     rows = pltpu.VMEM((ORDER, WIDE), F32)
+    edge = pltpu.VMEM((CHI, ORDER), BF)
+    here = pl.BlockSpec(memory_space=pltpu.HBM)
     a_mat, ket, bra, cols, turned, gwide = call(
         prepare_kernel,
         (
             shape(256, 256), shape(2, 256, 256), shape(2, 256, 256), shape(512, 256), shape(256, 512), shape(128, 2048),
         ),
-        [rows],
+        [rows, edge, edge, edge, pltpu.SemaphoreType.DMA((3,))],
         10**7, 2 * 10**6,
-    )(site, own_sketch, own_gtop, own_gleft)
-    sketched, downward, rightward, tops, first, lwide, second = call(
+        [pl.BlockSpec(memory_space=pltpu.VMEM), here, here, here],
+        room=PREP,
+    )(site, sketch[0, 0], grad_top[0, 0], grad_left[0, 0])
+    sketched, rightward, tops, first, lwide, second, quad = call(
         forward_kernel,
         (
-            shape(CHI, ORDER), shape(CHI, ORDER), shape(CHI, ORDER),
-            shape(512, WIDE), shape(512, WIDE), shape(WIDE, 2048), shape(256, 4096),
+            shape(CHI, ORDER), shape(CHI, ORDER),
+            shape(512, WIDE), shape(512, WIDE), shape(WIDE, 2048), shape(256, 4096), shape(512, 2048),
         ),
-        [rows, pltpu.VMEM((512, 2048), BF)],
+        [rows],
         2 * 10**9, 4 * 10**6,
-    )(corner_used, top_used, left_used, a_mat, turned, gwide)
-    sketch_below = from_behind(sketched, "row", -1)
-    sketch_beside = from_behind(sketched, "col", -1)
-    from_above = from_behind(downward, "row", 1)
-    from_left = from_behind(rightward, "col", 1)
-    grad_topped, grad_cornered, grad_lefted, dquad = call(
+    )(corner_used, top_used, left_used, a_mat, turned)
+    sketch_beside = from_behind(sketched, 0, -1)
+    sketch_below = from_behind(sketched, -1, 0)
+    from_left = from_behind(rightward, 0, 1)
+    downward = call(downward_kernel, shape(CHI, ORDER), [rows], 3 * 10**8, 3 * 10**6)(quad, gwide)
+    from_above = from_behind(downward, 1, 0)
+    part = call(
+        partial_kernel, shape(512, 2048, dtype=F32),
+        [rows, pltpu.VMEM((512, 256), BF), pltpu.VMEM((256, 2048), BF)],
+        5 * 10**8, 5 * 10**6,
+    )(sketch_below, sketch_beside, cols, gwide)
+    grad_lefted, dquad, dsecond = call(
         backward_kernel,
-        (shape(CHI, ORDER), shape(CHI, CHI), shape(CHI, ORDER), shape(256, 4096)),
-        [rows, pltpu.VMEM((512, 384), BF), pltpu.VMEM((384, 2048), BF), pltpu.VMEM((512, 2048), BF)],
-        3 * 10**9, 6 * 10**6,
-    )(sketch_below, sketch_beside, from_above, from_left, cols, gwide, a_mat, tops, first, lwide, corner_used)
-    top_result, corner_mid = from_behind((grad_topped, grad_cornered), "row", -1)
-    left_result, corner_result = from_behind((grad_lefted, corner_mid), "col", -1)
-    site_result = call(
-        site_kernel, shape(2, DD, DD, dtype=F32), [], 10**9, 5 * 10**6
-    )(dquad, second, ket, bra)
+        (shape(CHI, ORDER), shape(256, 4096), shape(512, 2048)),
+        [pltpu.VMEM((128, 2048), BF)],
+        2 * 10**9, 8 * 10**6,
+    )(from_above, from_left, part, cols, a_mat, first)
+    left_result = from_behind(grad_lefted, 0, -1)
+    grad_topped, grad_cornered = call(
+        edges_kernel, (shape(CHI, ORDER), shape(CHI, CHI)), [rows], 3 * 10**8, 3 * 10**6
+    )(dsecond, lwide, tops, corner_used)
+    top_result = from_behind(grad_topped, -1, 0)
+    corner_result = from_behind(grad_cornered, -1, -1)
+    site_result = call(site_kernel, shape(2, DD, DD, dtype=F32), [], 10**9, 5 * 10**6)(dquad, second, ket, bra)
+    corner_result, top_result, left_result = call(
+        finish_kernel,
+        (shape(CHI, CHI), shape(CHI, ORDER), shape(CHI, ORDER)),
+        [pltpu.SemaphoreType.DMA((3,))],
+        0, 6 * 10**5,
+        [pl.BlockSpec(memory_space=pltpu.VMEM)] * 3,
+        (here, here, here),
+    )(corner_result, top_result, left_result)
     return (
         corner_result[None, None],
         top_result[None, None],
@@ -296,7 +364,7 @@
     flat = P("row", "col", None, None)
     deep = P("row", "col", None, None, None, None, None)
     return jax.shard_map(
-        local,
+        step,
         mesh=mesh,
         in_specs=(flat, flat, flat, deep, flat, flat, flat),
         out_specs=(flat, flat, flat, deep),

time: 57.5 us -> 48.2 us (0.84)
  waiting for transfers between devices: 13.5 us -> 4.71 us
  Pallas kernels: 14.2 us -> 17 us
  local copies, waits for them, and re-layouts: 6.23 us -> 4.32 us
  starting transfers between devices: 22.7 us -> 21.1 us
    ppermute x12 -> x10, waiting for transfers between devices: 13.5 us -> 4.71 us  [from_behind(): return lax.ppermute(value, ('row', 'col'), pairs)]
    pallas_call x4 -> x8, Pallas kernels: 14.2 us -> 17 us  [the longest x1 4 us: step(): call(forward_kernel, (shape(CHI, ORDER), shape(CHI, ORDER), shape(512, WI...]
    unnamed x9 -> x6, local copies, waits for them, and re-layouts: 4.62 us -> 2.71 us
    ppermute x12 -> x10, starting transfers between devices: 22.7 us -> 21.1 us  [from_behind(): return lax.ppermute(value, ('row', 'col'), pairs)]
  transfers between devices with their start and end apart: 12 -> 10, of which waited for: 4 -> 3; matrix products, arithmetic and copies ran while one was open for 3% -> 3% of each run, Pallas kernels for 7% -> 16%
where the time goes in v2:
time: 48.2 us; the launch traced here: 48 us
  starting transfers between devices  21.1 us (44%)
  Pallas kernels  17 us (35%)
  waiting for transfers between devices  4.71 us (10%)
  local copies, waits for them, and re-layouts  4.32 us (9%)
  between operations  0.87 us (2%)
    ppermute x10, starting transfers between devices, from_behind(): return lax.ppermute(value, ('row', 'col'), pairs)  21.1 us
    ppermute x10, waiting for transfers between devices, from_behind(): return lax.ppermute(value, ('row', 'col'), pairs)  4.71 us
    pallas_call x1, Pallas kernels, step(): call(forward_kernel, (shape(CHI, ORDER), shape(CHI, ORDER), shape(512, WI...  4 us
    pallas_call x1, Pallas kernels, step(): call(backward_kernel, (shape(CHI, ORDER), shape(256, 4096), shape(512, 20...  3.46 us
    unnamed x6, local copies, waits for them, and re-layouts  2.71 us
    pallas_call x1, Pallas kernels, step(): call(site_kernel, shape(2, DD, DD, dtype=F32), [], 10 ** 9, 5 * 10 ** 6)  2.54 us
    pallas_call x1, Pallas kernels, step(): call(prepare_kernel, (shape(256, 256), shape(2, 256, 256), shape(2, 256,...  2.11 us
    pallas_call x1, Pallas kernels, step(): call(partial_kernel, shape(512, 2048, dtype=F32), [rows, pltpu.VMEM((512,...  1.88 us
  transfers between devices with their start and end apart: 10, of which 3 were waited for; matrix products, arithmetic and copies ran while one was open for 3% of the time, Pallas kernels for 16%

profile of v2, /device:TPU:1, one launch (start us, length us, event | category | flops | bytes accessed | tf_op | source)
XLA Modules:
  0.0 48.0 jit_solution(6703029393892150792)
XLA Ops:
  0.6 2.1 %collective-permute-start.1 = (bf16[64,1024]{1,0:T(8,128)(2,1)}, bf16[64,1024]{1,0:T(8,128)(2,1)S(1)}, u32[]{:S(2)}, u32[]{:S(2)}) collective-permute-start(bf16[64,1024]{1,0:T(8,128)(2,1)} %bitcast.12), channel_id=1, source_target_pairs={{0,16},{1,17},{2,18},{3,19},{4,20},{5,21},{6,22},{7,23},{8,24},{9,... | collective-permute-start | bytes 393224 | tf_op jit(solution)/shard_map/ppermute | solution.py:294
  2.7 3.3 %collective-permute-start.2 = (bf16[64,1024]{1,0:T(8,128)(2,1)}, bf16[64,1024]{1,0:T(8,128)(2,1)S(1)}, u32[]{:S(2)}, u32[]{:S(2)}) collective-permute-start(bf16[64,1024]{1,0:T(8,128)(2,1)} %bitcast.13), channel_id=1, source_target_pairs={{0,1},{1,2},{2,3},{3,4},{4,5},{5,6},{6,7},{7,8},{8,9},{9,10},{10,1... | collective-permute-start | bytes 393224 | tf_op jit(solution)/shard_map/ppermute | solution.py:294
  6.0 0.7 %collective-permute-start = (bf16[64,64]{1,0:T(8,128)(2,1)}, bf16[64,64]{1,0:T(8,128)(2,1)S(1)}, u32[]{:S(2)}, u32[]{:S(2)}) collective-permute-start(bf16[64,64]{1,0:T(8,128)(2,1)} %bitcast.16), channel_id=1, source_target_pairs={{0,17},{1,18},{2,19},{3,20},{4,21},{5,22},{6,23},{7,24},{8,25},{9,... | collective-permute-start | bytes 24584 | tf_op jit(solution)/shard_map/ppermute | solution.py:294
  6.8 0.8 %reshape.14.site_ref = bf16[2,16,16]{2,1,0:T(8,128)(2,1)S(1)} reshape(bf16[1,1,2,4,4,4,4]{6,5,4,3,2,1,0:T(4,128)(2,1)} %param.10) | data formatting | bytes 2048 | tf_op jit(solution)/shard_map/reshape | solution.py:298
  7.6 0.0 copy-start
  7.6 0.9 %copy-done = bf16[1,1,64,1024]{3,2,1,0:T(8,128)(2,1)S(1)} copy-done((bf16[1,1,64,1024]{3,2,1,0:T(8,128)(2,1)S(1)}, bf16[1,1,64,1024]{3,2,1,0:T(8,128)(2,1)}, u32[]{:S(2)}) %copy-start) | copy-done | bytes 131096
  8.5 0.9 %copy-done.1 = bf16[1,1,64,1024]{3,2,1,0:T(8,128)(2,1)S(1)} copy-done((bf16[1,1,64,1024]{3,2,1,0:T(8,128)(2,1)S(1)}, bf16[1,1,64,1024]{3,2,1,0:T(8,128)(2,1)}, u32[]{:S(2)}) %copy-start.1) | copy-done | bytes 131096
  9.4 0.9 %copy-done.2 = bf16[1,1,64,1024]{3,2,1,0:T(8,128)(2,1)S(1)} copy-done((bf16[1,1,64,1024]{3,2,1,0:T(8,128)(2,1)S(1)}, bf16[1,1,64,1024]{3,2,1,0:T(8,128)(2,1)}, u32[]{:S(2)}) %copy-start.2) | copy-done | bytes 131096
  10.3 2.1 %shard_map.102 = (bf16[256,256]{1,0:T(8,128)(2,1)S(1)}, bf16[2,256,256]{2,1,0:T(8,128)(2,1)S(1)}, bf16[2,256,256]{2,1,0:T(8,128)(2,1)S(1)}, bf16[512,256]{1,0:T(...) custom-call(bf16[2,16,16]{2,1,0:T(8,128)(2,1)S(1)} %reshape.14.site_ref, ...), custom_call_target="tpu_custom_call" | custom-call | flops 10000000 | bytes 2000000 | tf_op jit(solution)/shard_map/pallas_call | solution.py:305
  12.4 0.3 collective-permute-done.corner_ref
  12.7 0.0 collective-permute-done.1.top_ref
  12.7 0.0 collective-permute-done.2.left_ref
  12.7 4.0 %shard_map.103 = (bf16[64,1024]{1,0:T(8,128)(2,1)S(1)}, bf16[64,1024]{1,0:T(8,128)(2,1)S(1)}, bf16[512,128]{1,0:T(8,128)(2,1)S(1)}, bf16[512,128]{1,0:T(8,128)(2...) custom-call(bf16[64,64]{1,0:T(8,128)(2,1)S(1)} %collective-permute-done.corner_, ...), custom_call_target="tpu_custom_call" | custom-call | flops 2000000000 | bytes 4000000 | tf_op jit(solution)/shard_map/pallas_call | solution.py:315
  16.7 3.3 %collective-permute-start.6 = (bf16[64,1024]{1,0:T(8,128)(2,1)S(1)}, bf16[64,1024]{1,0:T(8,128)(2,1)S(1)}, u32[]{:S(2)}, u32[]{:S(2)}) collective-permute-start(bf16[64,1024]{1,0:T(8,128)(2,1)S(1)} %get-tuple-element.30), channel_id=1, source_target_pairs={{0,15},{1,0},{2,1},{3,2},{4,3},{5,4},{6,5},{7,6},{8,7},{9,8},{10,9... | collective-permute-start | bytes 393224 | tf_op jit(solution)/shard_map/ppermute | solution.py:294
  20.0 4.1 %collective-permute-start.5 = (bf16[64,1024]{1,0:T(8,128)(2,1)S(1)}, bf16[64,1024]{1,0:T(8,128)(2,1)S(1)}, u32[]{:S(2)}, u32[]{:S(2)}) collective-permute-start(bf16[64,1024]{1,0:T(8,128)(2,1)S(1)} %get-tuple-element.30), channel_id=1, source_target_pairs={{0,240},{1,241},{2,242},{3,243},{4,244},{5,245},{6,246},{7,247},{8... | collective-permute-start | bytes 393224 | tf_op jit(solution)/shard_map/ppermute | solution.py:294
  24.1 1.1 %shard_map.104 = bf16[64,1024]{1,0:T(8,128)(2,1)S(1)} custom-call(bf16[512,2048]{1,0:T(8,128)(2,1)S(1)} %get-tuple-element.27.quad_ref, bf16[128,2048]{1,0:T(8,128)(2,1)S(1)} %get-tuple-element.28.gwide_ref), custom_call_target="tpu_custom_call" | custom-call | flops 300000000 | bytes 3000000 | tf_op jit(solution)/shard_map/pallas_call | solution.py:327
  25.2 0.1 collective-permute-start.3
  25.3 0.5 collective-permute-start.4
  25.8 1.1 %collective-permute-done.5.below_ref = bf16[64,1024]{1,0:T(8,128)(2,1)S(1)} collective-permute-done((bf16[64,1024]{1,0:T(8,128)(2,1)S(1)}, bf16[64,1024]{1,0:T(8,128)(2,1)S(1)}, u32[]{:S(2)}, u32[]{:S(2)}) %collective-permute-start.5) | collective-permute-done | bytes 131104 | tf_op jit(solution)/shard_map/ppermute | solution.py:294
  26.8 1.9 %shard_map.105.part_ref = f32[512,2048]{1,0:T(8,128)S(1)} custom-call(bf16[64,1024]{1,0:T(8,128)(2,1)S(1)} %collective-permute-done.5.below_ref, bf16[64,1024]{1,0:T(8,128)(2,1)S(1)} %collective-permute-done.6.beside_ref, bf16[512,256]{1,0:T(8,128)(2,1)S(1)} %get-tuple-element.31.cols_ref, bf16[128,2048]{1,0:T(8,128)(2,1)S(1)} %get-tuple-element.28.gwide_ref), custom_call_target="tpu_custom_call" | custom-call | flops 500000000 | bytes 5000000 | tf_op jit(solution)/shard_map/pallas_call | solution.py:329
  28.7 3.3 %collective-permute-done.3.above_ref = bf16[64,1024]{1,0:T(8,128)(2,1)S(1)} collective-permute-done((bf16[64,1024]{1,0:T(8,128)(2,1)S(1)}, bf16[64,1024]{1,0:T(8,128)(2,1)S(1)}, u32[]{:S(2)}, u32[]{:S(2)}) %collective-permute-start.3) | collective-permute-done | bytes 131104 | tf_op jit(solution)/shard_map/ppermute | solution.py:294
  32.1 3.5 %shard_map.106 = (bf16[64,1024]{1,0:T(8,128)(2,1)S(1)}, bf16[256,4096]{1,0:T(8,128)(2,1)S(1)}, bf16[512,2048]{1,0:T(8,128)(2,1)S(1)}) custom-call(bf16[64,1024]{1,0:T(8,128)(2,1)S(1)} %collective-permute-done.3.above_ref, bf16[64,1024]{1,0:T(8,128)(2,1)S(1)} %collective-permute-done.4.behind_ref, f32[512,2048]{1,0:T(8,128)S(1)} %shard_map.105.part_ref, ...), custom_call_target="tpu_custom_call" | custom-call | flops 2000000000 | bytes 8000000 | tf_op jit(solution)/shard_map/pallas_call | solution.py:334
  35.5 1.2 %shard_map.107 = (bf16[64,1024]{1,0:T(8,128)(2,1)S(1)}, bf16[64,64]{1,0:T(8,128)(2,1)S(1)}) custom-call(bf16[512,2048]{1,0:T(8,128)(2,1)S(1)} %get-tuple-element.33.dsecond_ref, bf16[128,2048]{1,0:T(8,128)(2,1)S(1)} %get-tuple-element.34.lwide_ref, bf16[512,128]{1,0:T(8,128)(2,1)S(1)} %get-tuple-element.35.tops_ref, ...), custom_call_target="tpu_custom_call" | custom-call | flops 300000000 | bytes 3000000 | tf_op jit(solution)/shard_map/pallas_call | solution.py:341
  36.8 2.0 %collective-permute-start.8 = (bf16[64,1024]{1,0:T(8,128)(2,1)S(1)}, bf16[64,1024]{1,0:T(8,128)(2,1)S(1)}, u32[]{:S(2)}, u32[]{:S(2)}) collective-permute-start(bf16[64,1024]{1,0:T(8,128)(2,1)S(1)} %get-tuple-element.37), channel_id=1, source_target_pairs={{0,240},{1,241},{2,242},{3,243},{4,244},{5,245},{6,246},{7,247},{8... | collective-permute-start | bytes 393224 | tf_op jit(solution)/shard_map/ppermute | solution.py:294
  38.8 3.9 %collective-permute-start.9 = (bf16[64,1024]{1,0:T(8,128)(2,1)S(1)}, bf16[64,1024]{1,0:T(8,128)(2,1)S(1)}, u32[]{:S(2)}, u32[]{:S(2)}) collective-permute-start(bf16[64,1024]{1,0:T(8,128)(2,1)S(1)} %get-tuple-element.38), channel_id=1, source_target_pairs={{0,15},{1,0},{2,1},{3,2},{4,3},{5,4},{6,5},{7,6},{8,7},{9,8},{10,9... | collective-permute-start | bytes 393224 | tf_op jit(solution)/shard_map/ppermute | solution.py:294
  42.7 1.0 %collective-permute-start.7 = (bf16[64,64]{1,0:T(8,128)(2,1)S(1)}, bf16[64,64]{1,0:T(8,128)(2,1)S(1)}, u32[]{:S(2)}, u32[]{:S(2)}) collective-permute-start(bf16[64,64]{1,0:T(8,128)(2,1)S(1)} %get-tuple-element.36), channel_id=1, source_target_pairs={{0,255},{1,240},{2,241},{3,242},{4,243},{5,244},{6,245},{7,246},{8... | collective-permute-start | bytes 24584 | tf_op jit(solution)/shard_map/ppermute | solution.py:294
  43.8 2.5 %shard_map.109 = f32[2,16,16]{2,1,0:T(8,128)S(1)} custom-call(bf16[256,4096]{1,0:T(8,128)(2,1)S(1)} %get-tuple-element.42.dquad_ref, bf16[256,4096]{1,0:T(8,128)(2,1)S(1)} %get-tuple-element.43.second_ref, bf16[2,256,256]{2,1,0:T(8,128)(2,1)S(1)} %get-tuple-element.44.ket_ref, bf16[2,256,256]{2,1,0:T(8,128)(2,1)S(1)} %get-tuple-element.45.bra_ref), custom_call_target="tpu_custom_call" | custom-call | flops 1000000000 | bytes 5000000 | tf_op jit(solution)/shard_map/pallas_call | solution.py:346
  46.3 0.8 %reshape.15 = f32[1,1,2,4,4,4,4]{6,5,4,3,2,1,0:T(4,128)} reshape(f32[2,16,16]{2,1,0:T(8,128)S(1)} %shard_map.109) | data formatting | bytes 4096 | tf_op jit(solution)/shard_map/reshape | solution.py:359
  47.1 0.0 collective-permute-done.7.corner_ref
  47.1 0.0 collective-permute-done.8.top_ref
  47.1 0.0 collective-permute-done.9.left_ref
  47.1 0.7 %shard_map.108 = (bf16[64,64]{1,0:T(8,128)(2,1)}, bf16[64,1024]{1,0:T(8,128)(2,1)}, bf16[64,1024]{1,0:T(8,128)(2,1)}) custom-call(bf16[64,64]{1,0:T(8,128)(2,1)S(1)} %collective-permute-done.7.corner_ref, bf16[64,1024]{1,0:T(8,128)(2,1)S(1)} %collective-permute-done.8.top_ref, bf16[64,1024]{1,0:T(8,128)(2,1)S(1)} %collective-permute-done.9.left_ref), custom_call_target="tpu_custom_call" | custom-call | bytes 600000 | tf_op jit(solution)/shard_map/pallas_call | solution.py:347
  (4 shorter events, 0.0 us)
Async XLA Ops:
  0.6 12.1 %collective-permute-start.1 = (bf16[64,1024]{1,0:T(8,128)(2,1)}, bf16[64,1024]{1,0:T(8,128)(2,1)S(1)}, u32[]{:S(2)}, u32[]{:S(2)}) collective-permute-start(bf16[64,1024]{1,0:T(8,128)(2,1)} %bitcast.12), channel_id=1, source_target_pairs={{0,16},{1,17},{2,18},{3,19},{4,20},{5,21},{6,22},{7,23},{8,24},{9,... | collective-permute-start | bytes 393224 | tf_op jit(solution)/shard_map/ppermute | solution.py:294
  2.7 10.0 %collective-permute-start.2 = (bf16[64,1024]{1,0:T(8,128)(2,1)}, bf16[64,1024]{1,0:T(8,128)(2,1)S(1)}, u32[]{:S(2)}, u32[]{:S(2)}) collective-permute-start(bf16[64,1024]{1,0:T(8,128)(2,1)} %bitcast.13), channel_id=1, source_target_pairs={{0,1},{1,2},{2,3},{3,4},{4,5},{5,6},{6,7},{7,8},{8,9},{9,10},{10,1... | collective-permute-start | bytes 393224 | tf_op jit(solution)/shard_map/ppermute | solution.py:294
  6.0 6.7 %collective-permute-start = (bf16[64,64]{1,0:T(8,128)(2,1)}, bf16[64,64]{1,0:T(8,128)(2,1)S(1)}, u32[]{:S(2)}, u32[]{:S(2)}) collective-permute-start(bf16[64,64]{1,0:T(8,128)(2,1)} %bitcast.16), channel_id=1, source_target_pairs={{0,17},{1,18},{2,19},{3,20},{4,21},{5,22},{6,23},{7,24},{8,25},{9,... | collective-permute-start | bytes 24584 | tf_op jit(solution)/shard_map/ppermute | solution.py:294
  7.6 0.9 %copy-start = (bf16[1,1,64,1024]{3,2,1,0:T(8,128)(2,1)S(1)}, bf16[1,1,64,1024]{3,2,1,0:T(8,128)(2,1)}, u32[]{:S(2)}) copy-start(bf16[1,1,64,1024]{3,2,1,0:T(8,128)(2,1)} %param.11) | copy-start | bytes 393220
  8.5 0.9 %copy-start.1 = (bf16[1,1,64,1024]{3,2,1,0:T(8,128)(2,1)S(1)}, bf16[1,1,64,1024]{3,2,1,0:T(8,128)(2,1)}, u32[]{:S(2)}) copy-start(bf16[1,1,64,1024]{3,2,1,0:T(8,128)(2,1)} %param.13) | copy-start | bytes 393220
  9.4 0.9 %copy-start.2 = (bf16[1,1,64,1024]{3,2,1,0:T(8,128)(2,1)S(1)}, bf16[1,1,64,1024]{3,2,1,0:T(8,128)(2,1)}, u32[]{:S(2)}) copy-start(bf16[1,1,64,1024]{3,2,1,0:T(8,128)(2,1)} %param.12) | copy-start | bytes 393220
  16.7 9.1 %collective-permute-start.6 = (bf16[64,1024]{1,0:T(8,128)(2,1)S(1)}, bf16[64,1024]{1,0:T(8,128)(2,1)S(1)}, u32[]{:S(2)}, u32[]{:S(2)}) collective-permute-start(bf16[64,1024]{1,0:T(8,128)(2,1)S(1)} %get-tuple-element.30), channel_id=1, source_target_pairs={{0,15},{1,0},{2,1},{3,2},{4,3},{5,4},{6,5},{7,6},{8,7},{9,8},{10,9... | collective-permute-start | bytes 393224 | tf_op jit(solution)/shard_map/ppermute | solution.py:294
  20.0 6.8 %collective-permute-start.5 = (bf16[64,1024]{1,0:T(8,128)(2,1)S(1)}, bf16[64,1024]{1,0:T(8,128)(2,1)S(1)}, u32[]{:S(2)}, u32[]{:S(2)}) collective-permute-start(bf16[64,1024]{1,0:T(8,128)(2,1)S(1)} %get-tuple-element.30), channel_id=1, source_target_pairs={{0,240},{1,241},{2,242},{3,243},{4,244},{5,245},{6,246},{7,247},{8... | collective-permute-start | bytes 393224 | tf_op jit(solution)/shard_map/ppermute | solution.py:294
  25.2 6.9 %collective-permute-start.3 = (bf16[64,1024]{1,0:T(8,128)(2,1)S(1)}, bf16[64,1024]{1,0:T(8,128)(2,1)S(1)}, u32[]{:S(2)}, u32[]{:S(2)}) collective-permute-start(bf16[64,1024]{1,0:T(8,128)(2,1)S(1)} %shard_map.104), channel_id=1, source_target_pairs={{0,16},{1,17},{2,18},{3,19},{4,20},{5,21},{6,22},{7,23},{8,24},{9,... | collective-permute-start | bytes 393224 | tf_op jit(solution)/shard_map/ppermute | solution.py:294
  25.3 6.8 %collective-permute-start.4 = (bf16[64,1024]{1,0:T(8,128)(2,1)S(1)}, bf16[64,1024]{1,0:T(8,128)(2,1)S(1)}, u32[]{:S(2)}, u32[]{:S(2)}) collective-permute-start(bf16[64,1024]{1,0:T(8,128)(2,1)S(1)} %get-tuple-element.29), channel_id=1, source_target_pairs={{0,1},{1,2},{2,3},{3,4},{4,5},{5,6},{6,7},{7,8},{8,9},{9,10},{10,1... | collective-permute-start | bytes 393224 | tf_op jit(solution)/shard_map/ppermute | solution.py:294
  36.8 10.3 %collective-permute-start.8 = (bf16[64,1024]{1,0:T(8,128)(2,1)S(1)}, bf16[64,1024]{1,0:T(8,128)(2,1)S(1)}, u32[]{:S(2)}, u32[]{:S(2)}) collective-permute-start(bf16[64,1024]{1,0:T(8,128)(2,1)S(1)} %get-tuple-element.37), channel_id=1, source_target_pairs={{0,240},{1,241},{2,242},{3,243},{4,244},{5,245},{6,246},{7,247},{8... | collective-permute-start | bytes 393224 | tf_op jit(solution)/shard_map/ppermute | solution.py:294
  38.8 8.3 %collective-permute-start.9 = (bf16[64,1024]{1,0:T(8,128)(2,1)S(1)}, bf16[64,1024]{1,0:T(8,128)(2,1)S(1)}, u32[]{:S(2)}, u32[]{:S(2)}) collective-permute-start(bf16[64,1024]{1,0:T(8,128)(2,1)S(1)} %get-tuple-element.38), channel_id=1, source_target_pairs={{0,15},{1,0},{2,1},{3,2},{4,3},{5,4},{6,5},{7,6},{8,7},{9,8},{10,9... | collective-permute-start | bytes 393224 | tf_op jit(solution)/shard_map/ppermute | solution.py:294
  42.7 4.4 %collective-permute-start.7 = (bf16[64,64]{1,0:T(8,128)(2,1)S(1)}, bf16[64,64]{1,0:T(8,128)(2,1)S(1)}, u32[]{:S(2)}, u32[]{:S(2)}) collective-permute-start(bf16[64,64]{1,0:T(8,128)(2,1)S(1)} %get-tuple-element.36), channel_id=1, source_target_pairs={{0,255},{1,240},{2,241},{3,242},{4,243},{5,244},{6,245},{7,246},{8... | collective-permute-start | bytes 24584 | tf_op jit(solution)/shard_map/ppermute | solution.py:294

commit v3 on v2

--- a/solution.py
+++ b/solution.py
@@ -37,8 +37,7 @@
 
 
 def to_rows(nat, rows_ref, out_ref, column):
-    value = nat.astype(F32)
-    rows_ref[...] = jnp.concatenate([value, value], axis=0).T
+    rows_ref[...] = jnp.concatenate([nat, nat], axis=0).T.astype(F32)
     low = first_half((DD, WIDE))
     for at in range(HALF):
         even = rows_ref[pl.ds(2 * at, DD, stride=CHI), :]
@@ -51,7 +50,7 @@
         tile = value[at * DD : (at + 1) * DD, :]
         rows_ref[pl.ds(2 * at, DD, stride=CHI), :] = tile
         rows_ref[pl.ds(2 * at + 1, DD, stride=CHI), :] = tile
-    turned = rows_ref[...].T
+    turned = rows_ref[...].astype(BF).T
     even = iota((CHI, ORDER), 1) % 2 == 0
     return jnp.where(even, turned[:CHI], turned[CHI:])
 
@@ -145,7 +144,7 @@
             second_ref[pl.ds(row + DD, DD), one * WIDE : (one + 1) * WIDE] = piece[:, WIDE:]
         return carry
 
-    lax.fori_loop(0, DD // 2, second_step, 0, unroll=2)
+    lax.fori_loop(0, DD // 2, second_step, 0, unroll=8)
 
     def quad_step(pair, carry):
         at = pl.multiple_of(pair * 2 * WIDE, 2 * WIDE)
@@ -157,7 +156,7 @@
             quad_ref[pl.ds(row + DD, DD), leg * WIDE : (leg + 1) * WIDE] = piece[:, WIDE:]
         return carry
 
-    lax.fori_loop(0, HALF // 2, quad_step, 0, unroll=4)
+    lax.fori_loop(0, HALF // 2, quad_step, 0, unroll=16)
 
     for pair in range(DD // 2):
         at = pair * 2 * WIDE
@@ -168,7 +167,7 @@
 
 def downward_kernel(quad_ref, gwide_ref, downward_ref, rows_ref):
     down = dot_nt(quad_ref[...], gwide_ref[...])
-    downward_ref[...] = from_rows(down, rows_ref).astype(BF)
+    downward_ref[...] = from_rows(down, rows_ref)
 
 
 def partial_kernel(below_ref, beside_ref, cols_ref, gwide_ref, part_ref, rows_ref, right_ref, left_ref):
@@ -182,7 +181,7 @@
         part_ref[:, pl.ds(at, 2 * WIDE)] = dot(right_ref[...], left_ref[:, pl.ds(at, 2 * WIDE)])
         return carry
 
-    lax.fori_loop(0, DD // 2, step, 0, unroll=2)
+    lax.fori_loop(0, DD // 2, step, 0, unroll=8)
 
 
 def backward_kernel(
@@ -204,7 +203,7 @@
             dquad_ref[pl.ds(row + DD, DD), one * WIDE : (one + 1) * WIDE] = piece[:, WIDE:]
         return carry
 
-    lax.fori_loop(0, DD // 2, dquad_step, 0, unroll=2)
+    lax.fori_loop(0, DD // 2, dquad_step, 0, unroll=8)
     a_turned = a_ref[...].T
 
     def dsecond_step(pair, carry):
@@ -217,7 +216,7 @@
             dsecond_ref[pl.ds(row + DD, DD), leg * WIDE : (leg + 1) * WIDE] = piece[:, WIDE:]
         return carry
 
-    lax.fori_loop(0, HALF // 2, dsecond_step, 0, unroll=4)
+    lax.fori_loop(0, HALF // 2, dsecond_step, 0, unroll=16)
 
     first_turned = first_ref[...].T
     for pair in range(DD // 2):
@@ -229,28 +228,23 @@
 def edges_kernel(dsecond_ref, lwide_ref, tops_ref, corner_ref, top_out_ref, corner_out_ref, rows_ref):
     dfirst = dot_nt(dsecond_ref[...], lwide_ref[...]).astype(BF)
     dtop = dot(dfirst, corner_pair(corner_ref[...]))
-    top_out_ref[...] = from_rows(dtop, rows_ref).astype(BF)
+    top_out_ref[...] = from_rows(dtop, rows_ref)
     dcorner = dot_tn(dfirst, tops_ref[...])
     corner_out_ref[...] = (dcorner[:CHI, :CHI] + pltpu.roll(dcorner[CHI:], CHI, 1)[:, :CHI]).astype(BF)
-
-
-def split(value):
-    high = value.astype(BF)
-    return high, (value - high.astype(F32)).astype(BF)
 
 
 def site_kernel(dquad_ref, second_ref, ket_ref, bra_ref, out_ref):
     grad = dot_nt(dquad_ref[...], second_ref[...])
     ket_map, bra_map = leg_maps()
-    for phys in range(2):
-        total = None
-        for other_ref, leg_map in ((ket_ref, bra_map), (bra_ref, ket_map)):
-            for part in split(grad * other_ref[phys].astype(F32)):
-                half = dot_nt(leg_map, part)
-                for piece in split(half):
-                    term = dot_nt(piece, leg_map)
-                    total = term if total is None else total + term
-        out_ref[phys] = total
+    total = None
+    for other_ref, leg_map in ((ket_ref, bra_map), (bra_ref, ket_map)):
+        pieces = [(grad * other_ref[phys].astype(F32)).astype(BF) for phys in range(2)]
+        half = dot_nt(jnp.concatenate(pieces, axis=0), leg_map).astype(BF)
+        term = dot(leg_map, jnp.concatenate([half[: 2 * WIDE], half[2 * WIDE :]], axis=1))
+        total = term if total is None else total + term
+    turned = total.T
+    out_ref[0] = turned[:DD]
+    out_ref[1] = turned[DD:]
 
 
 def finish_kernel(corner_ref, top_ref, left_ref, corner_hbm, top_hbm, left_hbm, sems):
@@ -282,6 +276,10 @@
         compiler_params=pltpu.CompilerParams(vmem_limit_bytes=room),
         cost_estimate=pl.CostEstimate(flops=flops, bytes_accessed=moved, transcendentals=0),
     )
+
+
+def in_hbm(shard):
+    return pltpu.with_memory_space_constraint(shard[0, 0], pltpu.HBM)
 
 
 def from_behind(value, down, right):
@@ -311,7 +309,7 @@
         10**7, 2 * 10**6,
         [pl.BlockSpec(memory_space=pltpu.VMEM), here, here, here],
         room=PREP,
-    )(site, sketch[0, 0], grad_top[0, 0], grad_left[0, 0])
+    )(site, in_hbm(sketch), in_hbm(grad_top), in_hbm(grad_left))
     sketched, rightward, tops, first, lwide, second, quad = call(
         forward_kernel,
         (

time: 48.2 us -> 45 us (0.934)
  waiting for transfers between devices: 4.71 us -> 10.4 us
  Pallas kernels: 17 us -> 12.4 us
  local copies, waits for them, and re-layouts: 4.32 us -> 1.58 us
  starting transfers between devices: 21.1 us -> 19.6 us
    ppermute x10, waiting for transfers between devices: 4.71 us -> 10.4 us  [from_behind(): return lax.ppermute(value, ('row', 'col'), pairs)]
    unnamed x6 -> x0, local copies, waits for them, and re-layouts: 2.71 us -> none
    pallas_call x1, Pallas kernels: 3.46 us -> 1.81 us  [step(): call(backward_kernel, (shape(CHI, ORDER), shape(256, 4096), shape(512, 20...]
    ppermute x10, starting transfers between devices: 21.1 us -> 19.6 us  [from_behind(): return lax.ppermute(value, ('row', 'col'), pairs)]
    pallas_call x1, Pallas kernels: 4 us -> 2.7 us  [step(): call(forward_kernel, (shape(CHI, ORDER), shape(CHI, ORDER), shape(512, WI...]
    pallas_call x1, Pallas kernels: 2.54 us -> 1.55 us  [step(): call(site_kernel, shape(2, DD, DD, dtype=F32), [], 10 ** 9, 5 * 10 ** 6)]
    pallas_call x1, Pallas kernels: 1.88 us -> 1.26 us  [step(): call(partial_kernel, shape(512, 2048, dtype=F32), [rows, pltpu.VMEM((512,...]
  transfers between devices with their start and end apart: 10 -> 10, of which waited for: 3 -> 4; matrix products, arithmetic and copies ran while one was open for 3% -> 4% of each run, Pallas kernels for 16% -> 13%
where the time goes in v3:
time: 45 us; the launch traced here: 44.9 us
  starting transfers between devices  19.6 us (44%)
  Pallas kernels  12.4 us (28%)
  waiting for transfers between devices  10.4 us (23%)
  local copies, waits for them, and re-layouts  1.58 us (4%)
  between operations  0.87 us (2%)
    ppermute x10, starting transfers between devices, from_behind(): return lax.ppermute(value, ('row', 'col'), pairs)  19.6 us
    ppermute x10, waiting for transfers between devices, from_behind(): return lax.ppermute(value, ('row', 'col'), pairs)  10.4 us
    pallas_call x1, Pallas kernels, step(): call(forward_kernel, (shape(CHI, ORDER), shape(CHI, ORDER), shape(512, WI...  2.7 us
    pallas_call x1, Pallas kernels, step(): call(prepare_kernel, (shape(256, 256), shape(2, 256, 256), shape(2, 256,...  2.01 us
    pallas_call x1, Pallas kernels, step(): call(backward_kernel, (shape(CHI, ORDER), shape(256, 4096), shape(512, 20...  1.81 us
    pallas_call x1, Pallas kernels, step(): call(site_kernel, shape(2, DD, DD, dtype=F32), [], 10 ** 9, 5 * 10 ** 6)  1.55 us
    pallas_call x1, Pallas kernels, step(): call(partial_kernel, shape(512, 2048, dtype=F32), [rows, pltpu.VMEM((512,...  1.26 us
    pallas_call x1, Pallas kernels, step(): call(edges_kernel, (shape(CHI, ORDER), shape(CHI, CHI)), [rows], 3 * 10 *...  1.22 us
  transfers between devices with their start and end apart: 10, of which 4 were waited for; matrix products, arithmetic and copies ran while one was open for 4% of the time, Pallas kernels for 13%

profile of v3, /device:TPU:1, one launch (start us, length us, event | category | flops | bytes accessed | tf_op | source)
XLA Modules:
  0.0 44.9 jit_solution(1070299379982188409)
XLA Ops:
  0.6 2.1 %collective-permute-start.1 = (bf16[64,1024]{1,0:T(8,128)(2,1)}, bf16[64,1024]{1,0:T(8,128)(2,1)S(1)}, u32[]{:S(2)}, u32[]{:S(2)}) collective-permute-start(bf16[64,1024]{1,0:T(8,128)(2,1)} %bitcast.12), channel_id=1, source_target_pairs={{0,16},{1,17},{2,18},{3,19},{4,20},{5,21},{6,22},{7,23},{8,24},{9,... | collective-permute-start | bytes 393224 | tf_op jit(solution)/shard_map/ppermute | solution.py:292
  2.7 3.3 %collective-permute-start.2 = (bf16[64,1024]{1,0:T(8,128)(2,1)}, bf16[64,1024]{1,0:T(8,128)(2,1)S(1)}, u32[]{:S(2)}, u32[]{:S(2)}) collective-permute-start(bf16[64,1024]{1,0:T(8,128)(2,1)} %bitcast.13), channel_id=1, source_target_pairs={{0,1},{1,2},{2,3},{3,4},{4,5},{5,6},{6,7},{7,8},{8,9},{9,10},{10,1... | collective-permute-start | bytes 393224 | tf_op jit(solution)/shard_map/ppermute | solution.py:292
  6.0 0.7 %collective-permute-start = (bf16[64,64]{1,0:T(8,128)(2,1)}, bf16[64,64]{1,0:T(8,128)(2,1)S(1)}, u32[]{:S(2)}, u32[]{:S(2)}) collective-permute-start(bf16[64,64]{1,0:T(8,128)(2,1)} %bitcast.16), channel_id=1, source_target_pairs={{0,17},{1,18},{2,19},{3,20},{4,21},{5,22},{6,23},{7,24},{8,25},{9,... | collective-permute-start | bytes 24584 | tf_op jit(solution)/shard_map/ppermute | solution.py:292
  6.8 0.8 %reshape.14.site_ref = bf16[2,16,16]{2,1,0:T(8,128)(2,1)S(1)} reshape(bf16[1,1,2,4,4,4,4]{6,5,4,3,2,1,0:T(4,128)(2,1)} %param.10) | data formatting | bytes 2048 | tf_op jit(solution)/shard_map/reshape | solution.py:296
  7.6 2.0 %shard_map.102 = (bf16[256,256]{1,0:T(8,128)(2,1)S(1)}, bf16[2,256,256]{2,1,0:T(8,128)(2,1)S(1)}, bf16[2,256,256]{2,1,0:T(8,128)(2,1)S(1)}, bf16[512,256]{1,0:T(...) custom-call(bf16[2,16,16]{2,1,0:T(8,128)(2,1)S(1)} %reshape.14.site_ref, ...), custom_call_target="tpu_custom_call" | custom-call | flops 10000000 | bytes 2000000 | tf_op jit(solution)/shard_map/pallas_call | solution.py:303
  9.6 3.1 %collective-permute-done.corner_ref = bf16[64,64]{1,0:T(8,128)(2,1)S(1)} collective-permute-done((bf16[64,64]{1,0:T(8,128)(2,1)}, bf16[64,64]{1,0:T(8,128)(2,1)S(1)}, u32[]{:S(2)}, u32[]{:S(2)}) %collective-permute-start) | collective-permute-done | bytes 8224 | tf_op jit(solution)/shard_map/ppermute | solution.py:292
  12.7 0.0 collective-permute-done.1.top_ref
  12.7 0.0 collective-permute-done.2.left_ref
  12.7 2.7 %shard_map.103 = (bf16[64,1024]{1,0:T(8,128)(2,1)S(1)}, bf16[64,1024]{1,0:T(8,128)(2,1)S(1)}, bf16[512,128]{1,0:T(8,128)(2,1)S(1)}, bf16[512,128]{1,0:T(8,128)(2...) custom-call(bf16[64,64]{1,0:T(8,128)(2,1)S(1)} %collective-permute-done.corner_, ...), custom_call_target="tpu_custom_call" | custom-call | flops 2000000000 | bytes 4000000 | tf_op jit(solution)/shard_map/pallas_call | solution.py:313
  15.4 3.3 %collective-permute-start.6 = (bf16[64,1024]{1,0:T(8,128)(2,1)S(1)}, bf16[64,1024]{1,0:T(8,128)(2,1)S(1)}, u32[]{:S(2)}, u32[]{:S(2)}) collective-permute-start(bf16[64,1024]{1,0:T(8,128)(2,1)S(1)} %get-tuple-element.30), channel_id=1, source_target_pairs={{0,15},{1,0},{2,1},{3,2},{4,3},{5,4},{6,5},{7,6},{8,7},{9,8},{10,9... | collective-permute-start | bytes 393224 | tf_op jit(solution)/shard_map/ppermute | solution.py:292
  18.7 4.1 %collective-permute-start.5 = (bf16[64,1024]{1,0:T(8,128)(2,1)S(1)}, bf16[64,1024]{1,0:T(8,128)(2,1)S(1)}, u32[]{:S(2)}, u32[]{:S(2)}) collective-permute-start(bf16[64,1024]{1,0:T(8,128)(2,1)S(1)} %get-tuple-element.30), channel_id=1, source_target_pairs={{0,240},{1,241},{2,242},{3,243},{4,244},{5,245},{6,246},{7,247},{8... | collective-permute-start | bytes 393224 | tf_op jit(solution)/shard_map/ppermute | solution.py:292
  22.8 1.1 %shard_map.104 = bf16[64,1024]{1,0:T(8,128)(2,1)S(1)} custom-call(bf16[512,2048]{1,0:T(8,128)(2,1)S(1)} %get-tuple-element.27.quad_ref, bf16[128,2048]{1,0:T(8,128)(2,1)S(1)} %get-tuple-element.28.gwide_ref), custom_call_target="tpu_custom_call" | custom-call | flops 300000000 | bytes 3000000 | tf_op jit(solution)/shard_map/pallas_call | solution.py:325
  23.9 0.1 collective-permute-start.3
  24.0 0.3 collective-permute-start.4
  24.2 0.0 collective-permute-done.6.beside_ref
  24.3 1.3 %collective-permute-done.5.below_ref = bf16[64,1024]{1,0:T(8,128)(2,1)S(1)} collective-permute-done((bf16[64,1024]{1,0:T(8,128)(2,1)S(1)}, bf16[64,1024]{1,0:T(8,128)(2,1)S(1)}, u32[]{:S(2)}, u32[]{:S(2)}) %collective-permute-start.5) | collective-permute-done | bytes 131104 | tf_op jit(solution)/shard_map/ppermute | solution.py:292
  25.5 1.3 %shard_map.105.part_ref = f32[512,2048]{1,0:T(8,128)S(1)} custom-call(bf16[64,1024]{1,0:T(8,128)(2,1)S(1)} %collective-permute-done.5.below_ref, bf16[64,1024]{1,0:T(8,128)(2,1)S(1)} %collective-permute-done.6.beside_ref, bf16[512,256]{1,0:T(8,128)(2,1)S(1)} %get-tuple-element.31.cols_ref, bf16[128,2048]{1,0:T(8,128)(2,1)S(1)} %get-tuple-element.28.gwide_ref), custom_call_target="tpu_custom_call" | custom-call | flops 500000000 | bytes 5000000 | tf_op jit(solution)/shard_map/pallas_call | solution.py:327
  26.8 3.9 %collective-permute-done.3.above_ref = bf16[64,1024]{1,0:T(8,128)(2,1)S(1)} collective-permute-done((bf16[64,1024]{1,0:T(8,128)(2,1)S(1)}, bf16[64,1024]{1,0:T(8,128)(2,1)S(1)}, u32[]{:S(2)}, u32[]{:S(2)}) %collective-permute-start.3) | collective-permute-done | bytes 131104 | tf_op jit(solution)/shard_map/ppermute | solution.py:292
  30.8 0.0 collective-permute-done.4.behind_ref
  30.8 1.8 %shard_map.106 = (bf16[64,1024]{1,0:T(8,128)(2,1)S(1)}, bf16[256,4096]{1,0:T(8,128)(2,1)S(1)}, bf16[512,2048]{1,0:T(8,128)(2,1)S(1)}) custom-call(bf16[64,1024]{1,0:T(8,128)(2,1)S(1)} %collective-permute-done.3.above_ref, bf16[64,1024]{1,0:T(8,128)(2,1)S(1)} %collective-permute-done.4.behind_ref, f32[512,2048]{1,0:T(8,128)S(1)} %shard_map.105.part_ref, ...), custom_call_target="tpu_custom_call" | custom-call | flops 2000000000 | bytes 8000000 | tf_op jit(solution)/shard_map/pallas_call | solution.py:332
  32.6 1.2 %shard_map.107 = (bf16[64,1024]{1,0:T(8,128)(2,1)S(1)}, bf16[64,64]{1,0:T(8,128)(2,1)S(1)}) custom-call(bf16[512,2048]{1,0:T(8,128)(2,1)S(1)} %get-tuple-element.33.dsecond_ref, bf16[128,2048]{1,0:T(8,128)(2,1)S(1)} %get-tuple-element.34.lwide_ref, bf16[512,128]{1,0:T(8,128)(2,1)S(1)} %get-tuple-element.35.tops_ref, ...), custom_call_target="tpu_custom_call" | custom-call | flops 300000000 | bytes 3000000 | tf_op jit(solution)/shard_map/pallas_call | solution.py:339
  33.8 1.8 %collective-permute-start.8 = (bf16[64,1024]{1,0:T(8,128)(2,1)S(1)}, bf16[64,1024]{1,0:T(8,128)(2,1)S(1)}, u32[]{:S(2)}, u32[]{:S(2)}) collective-permute-start(bf16[64,1024]{1,0:T(8,128)(2,1)S(1)} %get-tuple-element.37), channel_id=1, source_target_pairs={{0,240},{1,241},{2,242},{3,243},{4,244},{5,245},{6,246},{7,247},{8... | collective-permute-start | bytes 393224 | tf_op jit(solution)/shard_map/ppermute | solution.py:292
  35.6 4.0 %collective-permute-start.9 = (bf16[64,1024]{1,0:T(8,128)(2,1)S(1)}, bf16[64,1024]{1,0:T(8,128)(2,1)S(1)}, u32[]{:S(2)}, u32[]{:S(2)}) collective-permute-start(bf16[64,1024]{1,0:T(8,128)(2,1)S(1)} %get-tuple-element.38), channel_id=1, source_target_pairs={{0,15},{1,0},{2,1},{3,2},{4,3},{5,4},{6,5},{7,6},{8,7},{9,8},{10,9... | collective-permute-start | bytes 393224 | tf_op jit(solution)/shard_map/ppermute | solution.py:292
  39.6 0.0 collective-permute-start.7
  39.6 1.6 %shard_map.109 = f32[2,16,16]{2,1,0:T(8,128)S(1)} custom-call(bf16[256,4096]{1,0:T(8,128)(2,1)S(1)} %get-tuple-element.42.dquad_ref, bf16[256,4096]{1,0:T(8,128)(2,1)S(1)} %get-tuple-element.43.second_ref, bf16[2,256,256]{2,1,0:T(8,128)(2,1)S(1)} %get-tuple-element.44.ket_ref, bf16[2,256,256]{2,1,0:T(8,128)(2,1)S(1)} %get-tuple-element.45.bra_ref), custom_call_target="tpu_custom_call" | custom-call | flops 1000000000 | bytes 5000000 | tf_op jit(solution)/shard_map/pallas_call | solution.py:344
  41.1 0.7 %reshape.15 = f32[1,1,2,4,4,4,4]{6,5,4,3,2,1,0:T(4,128)} reshape(f32[2,16,16]{2,1,0:T(8,128)S(1)} %shard_map.109) | data formatting | bytes 4096 | tf_op jit(solution)/shard_map/reshape | solution.py:357
  41.9 2.1 %collective-permute-done.7.corner_ref = bf16[64,64]{1,0:T(8,128)(2,1)S(1)} collective-permute-done((bf16[64,64]{1,0:T(8,128)(2,1)S(1)}, bf16[64,64]{1,0:T(8,128)(2,1)S(1)}, u32[]{:S(2)}, u32[]{:S(2)}) %collective-permute-start.7) | collective-permute-done | bytes 8224 | tf_op jit(solution)/shard_map/ppermute | solution.py:292
  44.0 0.0 collective-permute-done.8.top_ref
  44.0 0.0 collective-permute-done.9.left_ref
  44.0 0.7 %shard_map.108 = (bf16[64,64]{1,0:T(8,128)(2,1)}, bf16[64,1024]{1,0:T(8,128)(2,1)}, bf16[64,1024]{1,0:T(8,128)(2,1)}) custom-call(bf16[64,64]{1,0:T(8,128)(2,1)S(1)} %collective-permute-done.7.corner_ref, bf16[64,1024]{1,0:T(8,128)(2,1)S(1)} %collective-permute-done.8.top_ref, bf16[64,1024]{1,0:T(8,128)(2,1)S(1)} %collective-permute-done.9.left_ref), custom_call_target="tpu_custom_call" | custom-call | bytes 600000 | tf_op jit(solution)/shard_map/pallas_call | solution.py:345
Async XLA Ops:
  0.6 12.1 %collective-permute-start.1 = (bf16[64,1024]{1,0:T(8,128)(2,1)}, bf16[64,1024]{1,0:T(8,128)(2,1)S(1)}, u32[]{:S(2)}, u32[]{:S(2)}) collective-permute-start(bf16[64,1024]{1,0:T(8,128)(2,1)} %bitcast.12), channel_id=1, source_target_pairs={{0,16},{1,17},{2,18},{3,19},{4,20},{5,21},{6,22},{7,23},{8,24},{9,... | collective-permute-start | bytes 393224 | tf_op jit(solution)/shard_map/ppermute | solution.py:292
  2.7 10.0 %collective-permute-start.2 = (bf16[64,1024]{1,0:T(8,128)(2,1)}, bf16[64,1024]{1,0:T(8,128)(2,1)S(1)}, u32[]{:S(2)}, u32[]{:S(2)}) collective-permute-start(bf16[64,1024]{1,0:T(8,128)(2,1)} %bitcast.13), channel_id=1, source_target_pairs={{0,1},{1,2},{2,3},{3,4},{4,5},{5,6},{6,7},{7,8},{8,9},{9,10},{10,1... | collective-permute-start | bytes 393224 | tf_op jit(solution)/shard_map/ppermute | solution.py:292
  6.0 6.7 %collective-permute-start = (bf16[64,64]{1,0:T(8,128)(2,1)}, bf16[64,64]{1,0:T(8,128)(2,1)S(1)}, u32[]{:S(2)}, u32[]{:S(2)}) collective-permute-start(bf16[64,64]{1,0:T(8,128)(2,1)} %bitcast.16), channel_id=1, source_target_pairs={{0,17},{1,18},{2,19},{3,20},{4,21},{5,22},{6,23},{7,24},{8,25},{9,... | collective-permute-start | bytes 24584 | tf_op jit(solution)/shard_map/ppermute | solution.py:292
  15.4 8.8 %collective-permute-start.6 = (bf16[64,1024]{1,0:T(8,128)(2,1)S(1)}, bf16[64,1024]{1,0:T(8,128)(2,1)S(1)}, u32[]{:S(2)}, u32[]{:S(2)}) collective-permute-start(bf16[64,1024]{1,0:T(8,128)(2,1)S(1)} %get-tuple-element.30), channel_id=1, source_target_pairs={{0,15},{1,0},{2,1},{3,2},{4,3},{5,4},{6,5},{7,6},{8,7},{9,8},{10,9... | collective-permute-start | bytes 393224 | tf_op jit(solution)/shard_map/ppermute | solution.py:292
  18.7 6.8 %collective-permute-start.5 = (bf16[64,1024]{1,0:T(8,128)(2,1)S(1)}, bf16[64,1024]{1,0:T(8,128)(2,1)S(1)}, u32[]{:S(2)}, u32[]{:S(2)}) collective-permute-start(bf16[64,1024]{1,0:T(8,128)(2,1)S(1)} %get-tuple-element.30), channel_id=1, source_target_pairs={{0,240},{1,241},{2,242},{3,243},{4,244},{5,245},{6,246},{7,247},{8... | collective-permute-start | bytes 393224 | tf_op jit(solution)/shard_map/ppermute | solution.py:292
  23.9 6.9 %collective-permute-start.3 = (bf16[64,1024]{1,0:T(8,128)(2,1)S(1)}, bf16[64,1024]{1,0:T(8,128)(2,1)S(1)}, u32[]{:S(2)}, u32[]{:S(2)}) collective-permute-start(bf16[64,1024]{1,0:T(8,128)(2,1)S(1)} %shard_map.104), channel_id=1, source_target_pairs={{0,16},{1,17},{2,18},{3,19},{4,20},{5,21},{6,22},{7,23},{8,24},{9,... | collective-permute-start | bytes 393224 | tf_op jit(solution)/shard_map/ppermute | solution.py:292
  24.0 6.8 %collective-permute-start.4 = (bf16[64,1024]{1,0:T(8,128)(2,1)S(1)}, bf16[64,1024]{1,0:T(8,128)(2,1)S(1)}, u32[]{:S(2)}, u32[]{:S(2)}) collective-permute-start(bf16[64,1024]{1,0:T(8,128)(2,1)S(1)} %get-tuple-element.29), channel_id=1, source_target_pairs={{0,1},{1,2},{2,3},{3,4},{4,5},{5,6},{6,7},{7,8},{8,9},{9,10},{10,1... | collective-permute-start | bytes 393224 | tf_op jit(solution)/shard_map/ppermute | solution.py:292
  33.8 10.2 %collective-permute-start.8 = (bf16[64,1024]{1,0:T(8,128)(2,1)S(1)}, bf16[64,1024]{1,0:T(8,128)(2,1)S(1)}, u32[]{:S(2)}, u32[]{:S(2)}) collective-permute-start(bf16[64,1024]{1,0:T(8,128)(2,1)S(1)} %get-tuple-element.37), channel_id=1, source_target_pairs={{0,240},{1,241},{2,242},{3,243},{4,244},{5,245},{6,246},{7,247},{8... | collective-permute-start | bytes 393224 | tf_op jit(solution)/shard_map/ppermute | solution.py:292
  35.6 8.3 %collective-permute-start.9 = (bf16[64,1024]{1,0:T(8,128)(2,1)S(1)}, bf16[64,1024]{1,0:T(8,128)(2,1)S(1)}, u32[]{:S(2)}, u32[]{:S(2)}) collective-permute-start(bf16[64,1024]{1,0:T(8,128)(2,1)S(1)} %get-tuple-element.38), channel_id=1, source_target_pairs={{0,15},{1,0},{2,1},{3,2},{4,3},{5,4},{6,5},{7,6},{8,7},{9,8},{10,9... | collective-permute-start | bytes 393224 | tf_op jit(solution)/shard_map/ppermute | solution.py:292
  39.6 4.4 %collective-permute-start.7 = (bf16[64,64]{1,0:T(8,128)(2,1)S(1)}, bf16[64,64]{1,0:T(8,128)(2,1)S(1)}, u32[]{:S(2)}, u32[]{:S(2)}) collective-permute-start(bf16[64,64]{1,0:T(8,128)(2,1)S(1)} %get-tuple-element.36), channel_id=1, source_target_pairs={{0,255},{1,240},{2,241},{3,242},{4,243},{5,244},{6,245},{7,246},{8... | collective-permute-start | bytes 24584 | tf_op jit(solution)/shard_map/ppermute | solution.py:292

commit v4 on v3

--- a/solution.py
+++ b/solution.py
@@ -13,6 +13,7 @@
 ORDER = DD * CHI
 HALF = CHI // 2
 WIDE = 2 * CHI
+LEAP = DD + 1
 PREP = 20 << 20
 
 
@@ -37,20 +38,23 @@
 
 
 def to_rows(nat, rows_ref, out_ref, column):
-    rows_ref[...] = jnp.concatenate([nat, nat], axis=0).T.astype(F32)
+    turned = jnp.concatenate([nat, nat], axis=0).T.astype(F32)
+    for leg in range(DD):
+        rows_ref[pl.ds(leg, CHI, stride=LEAP), :] = turned[leg * CHI : (leg + 1) * CHI]
     low = first_half((DD, WIDE))
     for at in range(HALF):
-        even = rows_ref[pl.ds(2 * at, DD, stride=CHI), :]
-        odd = rows_ref[pl.ds(2 * at + 1, DD, stride=CHI), :]
+        even = rows_ref[2 * at * LEAP : 2 * at * LEAP + DD, :]
+        odd = rows_ref[(2 * at + 1) * LEAP : (2 * at + 1) * LEAP + DD, :]
         out_ref[at * DD : (at + 1) * DD, column : column + WIDE] = jnp.where(low, even, odd).astype(BF)
 
 
 def from_rows(value, rows_ref):
     for at in range(HALF):
         tile = value[at * DD : (at + 1) * DD, :]
-        rows_ref[pl.ds(2 * at, DD, stride=CHI), :] = tile
-        rows_ref[pl.ds(2 * at + 1, DD, stride=CHI), :] = tile
-    turned = rows_ref[...].astype(BF).T
+        rows_ref[2 * at * LEAP : 2 * at * LEAP + DD, :] = tile
+        rows_ref[(2 * at + 1) * LEAP : (2 * at + 1) * LEAP + DD, :] = tile
+    legs = [rows_ref[pl.ds(leg, CHI, stride=LEAP), :].astype(BF) for leg in range(DD)]
+    turned = jnp.concatenate(legs, axis=0).T
     even = iota((CHI, ORDER), 1) % 2 == 0
     return jnp.where(even, turned[:CHI], turned[CHI:])
 
@@ -297,7 +301,7 @@
     left_used = from_behind(left_edge[0, 0], 0, 1)
     top_used = from_behind(top_edge[0, 0], 1, 0)
     corner_used = from_behind(corner[0, 0], 1, 1)
-    rows = pltpu.VMEM((ORDER, WIDE), F32)
+    rows = pltpu.VMEM((CHI * LEAP, WIDE), F32)
     edge = pltpu.VMEM((CHI, ORDER), BF)
     here = pl.BlockSpec(memory_space=pltpu.HBM)
     a_mat, ket, bra, cols, turned, gwide = call(

time: 45 us -> 44.4 us (0.987)
  Pallas kernels: 12.4 us -> 10.6 us
  waiting for transfers between devices: 10.4 us -> 11.4 us
    ppermute x10, waiting for transfers between devices: 10.4 us -> 11.4 us  [from_behind(): return lax.ppermute(value, ('row', 'col'), pairs)]
    pallas_call x1, Pallas kernels: 2.01 us -> 1.46 us  [step(): call(prepare_kernel, (shape(256, 256), shape(2, 256, 256), shape(2, 256,...]
  transfers between devices with their start and end apart: 10 -> 10, of which waited for: 4 -> 4; matrix products, arithmetic and copies ran while one was open for 4% -> 4% of each run, Pallas kernels for 13% -> 11%
where the time goes in v4:
time: 44.4 us; the launch traced here: 44.2 us
  starting transfers between devices  19.8 us (45%)
  waiting for transfers between devices  11.4 us (26%)
  Pallas kernels  10.6 us (24%)
  local copies, waits for them, and re-layouts  1.58 us (4%)
  between operations  0.87 us (2%)
    ppermute x10, starting transfers between devices, from_behind(): return lax.ppermute(value, ('row', 'col'), pairs)  19.8 us
    ppermute x10, waiting for transfers between devices, from_behind(): return lax.ppermute(value, ('row', 'col'), pairs)  11.4 us
    pallas_call x1, Pallas kernels, step(): call(forward_kernel, (shape(CHI, ORDER), shape(CHI, ORDER), shape(512, WI...  2.28 us
    pallas_call x1, Pallas kernels, step(): call(backward_kernel, (shape(CHI, ORDER), shape(256, 4096), shape(512, 20...  1.81 us
    pallas_call x1, Pallas kernels, step(): call(site_kernel, shape(2, DD, DD, dtype=F32), [], 10 ** 9, 5 * 10 ** 6)  1.55 us
    pallas_call x1, Pallas kernels, step(): call(prepare_kernel, (shape(256, 256), shape(2, 256, 256), shape(2, 256,...  1.46 us
    pallas_call x1, Pallas kernels, step(): call(edges_kernel, (shape(CHI, ORDER), shape(CHI, CHI)), [rows], 3 * 10 *...  1.05 us
  transfers between devices with their start and end apart: 10, of which 4 were waited for; matrix products, arithmetic and copies ran while one was open for 4% of the time, Pallas kernels for 11%

profile of v4, /device:TPU:1, one launch (start us, length us, event | category | flops | bytes accessed | tf_op | source)
XLA Modules:
  0.0 44.2 jit_solution(6767784355058911499)
XLA Ops:
  0.6 2.1 %collective-permute-start.1 = (bf16[64,1024]{1,0:T(8,128)(2,1)}, bf16[64,1024]{1,0:T(8,128)(2,1)S(1)}, u32[]{:S(2)}, u32[]{:S(2)}) collective-permute-start(bf16[64,1024]{1,0:T(8,128)(2,1)} %bitcast.12), channel_id=1, source_target_pairs={{0,16},{1,17},{2,18},{3,19},{4,20},{5,21},{6,22},{7,23},{8,24},{9,... | collective-permute-start | bytes 393224 | tf_op jit(solution)/shard_map/ppermute | solution.py:296
  2.7 3.3 %collective-permute-start.2 = (bf16[64,1024]{1,0:T(8,128)(2,1)}, bf16[64,1024]{1,0:T(8,128)(2,1)S(1)}, u32[]{:S(2)}, u32[]{:S(2)}) collective-permute-start(bf16[64,1024]{1,0:T(8,128)(2,1)} %bitcast.13), channel_id=1, source_target_pairs={{0,1},{1,2},{2,3},{3,4},{4,5},{5,6},{6,7},{7,8},{8,9},{9,10},{10,1... | collective-permute-start | bytes 393224 | tf_op jit(solution)/shard_map/ppermute | solution.py:296
  6.0 0.7 %collective-permute-start = (bf16[64,64]{1,0:T(8,128)(2,1)}, bf16[64,64]{1,0:T(8,128)(2,1)S(1)}, u32[]{:S(2)}, u32[]{:S(2)}) collective-permute-start(bf16[64,64]{1,0:T(8,128)(2,1)} %bitcast.16), channel_id=1, source_target_pairs={{0,17},{1,18},{2,19},{3,20},{4,21},{5,22},{6,23},{7,24},{8,25},{9,... | collective-permute-start | bytes 24584 | tf_op jit(solution)/shard_map/ppermute | solution.py:296
  6.8 0.8 %reshape.14.site_ref = bf16[2,16,16]{2,1,0:T(8,128)(2,1)S(1)} reshape(bf16[1,1,2,4,4,4,4]{6,5,4,3,2,1,0:T(4,128)(2,1)} %param.10) | data formatting | bytes 2048 | tf_op jit(solution)/shard_map/reshape | solution.py:300
  7.6 1.5 %shard_map.102 = (bf16[256,256]{1,0:T(8,128)(2,1)S(1)}, bf16[2,256,256]{2,1,0:T(8,128)(2,1)S(1)}, bf16[2,256,256]{2,1,0:T(8,128)(2,1)S(1)}, bf16[512,256]{1,0:T(...) custom-call(bf16[2,16,16]{2,1,0:T(8,128)(2,1)S(1)} %reshape.14.site_ref, ...), custom_call_target="tpu_custom_call" | custom-call | flops 10000000 | bytes 2000000 | tf_op jit(solution)/shard_map/pallas_call | solution.py:307
  9.1 3.6 %collective-permute-done.corner_ref = bf16[64,64]{1,0:T(8,128)(2,1)S(1)} collective-permute-done((bf16[64,64]{1,0:T(8,128)(2,1)}, bf16[64,64]{1,0:T(8,128)(2,1)S(1)}, u32[]{:S(2)}, u32[]{:S(2)}) %collective-permute-start) | collective-permute-done | bytes 8224 | tf_op jit(solution)/shard_map/ppermute | solution.py:296
  12.7 0.0 collective-permute-done.1.top_ref
  12.7 0.0 collective-permute-done.2.left_ref
  12.7 2.3 %shard_map.103 = (bf16[64,1024]{1,0:T(8,128)(2,1)S(1)}, bf16[64,1024]{1,0:T(8,128)(2,1)S(1)}, bf16[512,128]{1,0:T(8,128)(2,1)S(1)}, bf16[512,128]{1,0:T(8,128)(2...) custom-call(bf16[64,64]{1,0:T(8,128)(2,1)S(1)} %collective-permute-done.corner_, ...), custom_call_target="tpu_custom_call" | custom-call | flops 2000000000 | bytes 4000000 | tf_op jit(solution)/shard_map/pallas_call | solution.py:317
  15.0 3.3 %collective-permute-start.6 = (bf16[64,1024]{1,0:T(8,128)(2,1)S(1)}, bf16[64,1024]{1,0:T(8,128)(2,1)S(1)}, u32[]{:S(2)}, u32[]{:S(2)}) collective-permute-start(bf16[64,1024]{1,0:T(8,128)(2,1)S(1)} %get-tuple-element.30), channel_id=1, source_target_pairs={{0,15},{1,0},{2,1},{3,2},{4,3},{5,4},{6,5},{7,6},{8,7},{9,8},{10,9... | collective-permute-start | bytes 393224 | tf_op jit(solution)/shard_map/ppermute | solution.py:296
  18.3 4.1 %collective-permute-start.5 = (bf16[64,1024]{1,0:T(8,128)(2,1)S(1)}, bf16[64,1024]{1,0:T(8,128)(2,1)S(1)}, u32[]{:S(2)}, u32[]{:S(2)}) collective-permute-start(bf16[64,1024]{1,0:T(8,128)(2,1)S(1)} %get-tuple-element.30), channel_id=1, source_target_pairs={{0,240},{1,241},{2,242},{3,243},{4,244},{5,245},{6,246},{7,247},{8... | collective-permute-start | bytes 393224 | tf_op jit(solution)/shard_map/ppermute | solution.py:296
  22.4 0.8 %shard_map.104 = bf16[64,1024]{1,0:T(8,128)(2,1)S(1)} custom-call(bf16[512,2048]{1,0:T(8,128)(2,1)S(1)} %get-tuple-element.27.quad_ref, bf16[128,2048]{1,0:T(8,128)(2,1)S(1)} %get-tuple-element.28.gwide_ref), custom_call_target="tpu_custom_call" | custom-call | flops 300000000 | bytes 3000000 | tf_op jit(solution)/shard_map/pallas_call | solution.py:329
  23.2 0.1 collective-permute-start.3
  23.3 0.1 collective-permute-start.4
  23.4 0.0 collective-permute-done.6.beside_ref
  23.4 1.7 %collective-permute-done.5.below_ref = bf16[64,1024]{1,0:T(8,128)(2,1)S(1)} collective-permute-done((bf16[64,1024]{1,0:T(8,128)(2,1)S(1)}, bf16[64,1024]{1,0:T(8,128)(2,1)S(1)}, u32[]{:S(2)}, u32[]{:S(2)}) %collective-permute-start.5) | collective-permute-done | bytes 131104 | tf_op jit(solution)/shard_map/ppermute | solution.py:296
  25.1 0.9 %shard_map.105.part_ref = f32[512,2048]{1,0:T(8,128)S(1)} custom-call(bf16[64,1024]{1,0:T(8,128)(2,1)S(1)} %collective-permute-done.5.below_ref, bf16[64,1024]{1,0:T(8,128)(2,1)S(1)} %collective-permute-done.6.beside_ref, bf16[512,256]{1,0:T(8,128)(2,1)S(1)} %get-tuple-element.31.cols_ref, bf16[128,2048]{1,0:T(8,128)(2,1)S(1)} %get-tuple-element.28.gwide_ref), custom_call_target="tpu_custom_call" | custom-call | flops 500000000 | bytes 5000000 | tf_op jit(solution)/shard_map/pallas_call | solution.py:331
  26.0 4.1 %collective-permute-done.3.above_ref = bf16[64,1024]{1,0:T(8,128)(2,1)S(1)} collective-permute-done((bf16[64,1024]{1,0:T(8,128)(2,1)S(1)}, bf16[64,1024]{1,0:T(8,128)(2,1)S(1)}, u32[]{:S(2)}, u32[]{:S(2)}) %collective-permute-start.3) | collective-permute-done | bytes 131104 | tf_op jit(solution)/shard_map/ppermute | solution.py:296
  30.1 0.0 collective-permute-done.4.behind_ref
  30.1 1.8 %shard_map.106 = (bf16[64,1024]{1,0:T(8,128)(2,1)S(1)}, bf16[256,4096]{1,0:T(8,128)(2,1)S(1)}, bf16[512,2048]{1,0:T(8,128)(2,1)S(1)}) custom-call(bf16[64,1024]{1,0:T(8,128)(2,1)S(1)} %collective-permute-done.3.above_ref, bf16[64,1024]{1,0:T(8,128)(2,1)S(1)} %collective-permute-done.4.behind_ref, f32[512,2048]{1,0:T(8,128)S(1)} %shard_map.105.part_ref, ...), custom_call_target="tpu_custom_call" | custom-call | flops 2000000000 | bytes 8000000 | tf_op jit(solution)/shard_map/pallas_call | solution.py:336
  31.9 1.0 %shard_map.107 = (bf16[64,1024]{1,0:T(8,128)(2,1)S(1)}, bf16[64,64]{1,0:T(8,128)(2,1)S(1)}) custom-call(bf16[512,2048]{1,0:T(8,128)(2,1)S(1)} %get-tuple-element.33.dsecond_ref, bf16[128,2048]{1,0:T(8,128)(2,1)S(1)} %get-tuple-element.34.lwide_ref, bf16[512,128]{1,0:T(8,128)(2,1)S(1)} %get-tuple-element.35.tops_ref, ...), custom_call_target="tpu_custom_call" | custom-call | flops 300000000 | bytes 3000000 | tf_op jit(solution)/shard_map/pallas_call | solution.py:343
  32.9 1.8 %collective-permute-start.8 = (bf16[64,1024]{1,0:T(8,128)(2,1)S(1)}, bf16[64,1024]{1,0:T(8,128)(2,1)S(1)}, u32[]{:S(2)}, u32[]{:S(2)}) collective-permute-start(bf16[64,1024]{1,0:T(8,128)(2,1)S(1)} %get-tuple-element.37), channel_id=1, source_target_pairs={{0,240},{1,241},{2,242},{3,243},{4,244},{5,245},{6,246},{7,247},{8... | collective-permute-start | bytes 393224 | tf_op jit(solution)/shard_map/ppermute | solution.py:296
  34.7 4.2 %collective-permute-start.9 = (bf16[64,1024]{1,0:T(8,128)(2,1)S(1)}, bf16[64,1024]{1,0:T(8,128)(2,1)S(1)}, u32[]{:S(2)}, u32[]{:S(2)}) collective-permute-start(bf16[64,1024]{1,0:T(8,128)(2,1)S(1)} %get-tuple-element.38), channel_id=1, source_target_pairs={{0,15},{1,0},{2,1},{3,2},{4,3},{5,4},{6,5},{7,6},{8,7},{9,8},{10,9... | collective-permute-start | bytes 393224 | tf_op jit(solution)/shard_map/ppermute | solution.py:296
  38.9 0.2 collective-permute-start.7
  39.1 1.6 %shard_map.109 = f32[2,16,16]{2,1,0:T(8,128)S(1)} custom-call(bf16[256,4096]{1,0:T(8,128)(2,1)S(1)} %get-tuple-element.42.dquad_ref, bf16[256,4096]{1,0:T(8,128)(2,1)S(1)} %get-tuple-element.43.second_ref, bf16[2,256,256]{2,1,0:T(8,128)(2,1)S(1)} %get-tuple-element.44.ket_ref, bf16[2,256,256]{2,1,0:T(8,128)(2,1)S(1)} %get-tuple-element.45.bra_ref), custom_call_target="tpu_custom_call" | custom-call | flops 1000000000 | bytes 5000000 | tf_op jit(solution)/shard_map/pallas_call | solution.py:348
  40.6 0.7 %reshape.15 = f32[1,1,2,4,4,4,4]{6,5,4,3,2,1,0:T(4,128)} reshape(f32[2,16,16]{2,1,0:T(8,128)S(1)} %shard_map.109) | data formatting | bytes 4096 | tf_op jit(solution)/shard_map/reshape | solution.py:361
  41.4 1.9 %collective-permute-done.7.corner_ref = bf16[64,64]{1,0:T(8,128)(2,1)S(1)} collective-permute-done((bf16[64,64]{1,0:T(8,128)(2,1)S(1)}, bf16[64,64]{1,0:T(8,128)(2,1)S(1)}, u32[]{:S(2)}, u32[]{:S(2)}) %collective-permute-start.7) | collective-permute-done | bytes 8224 | tf_op jit(solution)/shard_map/ppermute | solution.py:296
  43.3 0.0 collective-permute-done.8.top_ref
  43.3 0.0 collective-permute-done.9.left_ref
  43.3 0.7 %shard_map.108 = (bf16[64,64]{1,0:T(8,128)(2,1)}, bf16[64,1024]{1,0:T(8,128)(2,1)}, bf16[64,1024]{1,0:T(8,128)(2,1)}) custom-call(bf16[64,64]{1,0:T(8,128)(2,1)S(1)} %collective-permute-done.7.corner_ref, bf16[64,1024]{1,0:T(8,128)(2,1)S(1)} %collective-permute-done.8.top_ref, bf16[64,1024]{1,0:T(8,128)(2,1)S(1)} %collective-permute-done.9.left_ref), custom_call_target="tpu_custom_call" | custom-call | bytes 600000 | tf_op jit(solution)/shard_map/pallas_call | solution.py:349
Async XLA Ops:
  0.6 12.1 %collective-permute-start.1 = (bf16[64,1024]{1,0:T(8,128)(2,1)}, bf16[64,1024]{1,0:T(8,128)(2,1)S(1)}, u32[]{:S(2)}, u32[]{:S(2)}) collective-permute-start(bf16[64,1024]{1,0:T(8,128)(2,1)} %bitcast.12), channel_id=1, source_target_pairs={{0,16},{1,17},{2,18},{3,19},{4,20},{5,21},{6,22},{7,23},{8,24},{9,... | collective-permute-start | bytes 393224 | tf_op jit(solution)/shard_map/ppermute | solution.py:296
  2.7 10.0 %collective-permute-start.2 = (bf16[64,1024]{1,0:T(8,128)(2,1)}, bf16[64,1024]{1,0:T(8,128)(2,1)S(1)}, u32[]{:S(2)}, u32[]{:S(2)}) collective-permute-start(bf16[64,1024]{1,0:T(8,128)(2,1)} %bitcast.13), channel_id=1, source_target_pairs={{0,1},{1,2},{2,3},{3,4},{4,5},{5,6},{6,7},{7,8},{8,9},{9,10},{10,1... | collective-permute-start | bytes 393224 | tf_op jit(solution)/shard_map/ppermute | solution.py:296
  6.0 6.7 %collective-permute-start = (bf16[64,64]{1,0:T(8,128)(2,1)}, bf16[64,64]{1,0:T(8,128)(2,1)S(1)}, u32[]{:S(2)}, u32[]{:S(2)}) collective-permute-start(bf16[64,64]{1,0:T(8,128)(2,1)} %bitcast.16), channel_id=1, source_target_pairs={{0,17},{1,18},{2,19},{3,20},{4,21},{5,22},{6,23},{7,24},{8,25},{9,... | collective-permute-start | bytes 24584 | tf_op jit(solution)/shard_map/ppermute | solution.py:296
  15.0 8.4 %collective-permute-start.6 = (bf16[64,1024]{1,0:T(8,128)(2,1)S(1)}, bf16[64,1024]{1,0:T(8,128)(2,1)S(1)}, u32[]{:S(2)}, u32[]{:S(2)}) collective-permute-start(bf16[64,1024]{1,0:T(8,128)(2,1)S(1)} %get-tuple-element.30), channel_id=1, source_target_pairs={{0,15},{1,0},{2,1},{3,2},{4,3},{5,4},{6,5},{7,6},{8,7},{9,8},{10,9... | collective-permute-start | bytes 393224 | tf_op jit(solution)/shard_map/ppermute | solution.py:296
  18.3 6.8 %collective-permute-start.5 = (bf16[64,1024]{1,0:T(8,128)(2,1)S(1)}, bf16[64,1024]{1,0:T(8,128)(2,1)S(1)}, u32[]{:S(2)}, u32[]{:S(2)}) collective-permute-start(bf16[64,1024]{1,0:T(8,128)(2,1)S(1)} %get-tuple-element.30), channel_id=1, source_target_pairs={{0,240},{1,241},{2,242},{3,243},{4,244},{5,245},{6,246},{7,247},{8... | collective-permute-start | bytes 393224 | tf_op jit(solution)/shard_map/ppermute | solution.py:296
  23.2 6.9 %collective-permute-start.3 = (bf16[64,1024]{1,0:T(8,128)(2,1)S(1)}, bf16[64,1024]{1,0:T(8,128)(2,1)S(1)}, u32[]{:S(2)}, u32[]{:S(2)}) collective-permute-start(bf16[64,1024]{1,0:T(8,128)(2,1)S(1)} %shard_map.104), channel_id=1, source_target_pairs={{0,16},{1,17},{2,18},{3,19},{4,20},{5,21},{6,22},{7,23},{8,24},{9,... | collective-permute-start | bytes 393224 | tf_op jit(solution)/shard_map/ppermute | solution.py:296
  23.3 6.8 %collective-permute-start.4 = (bf16[64,1024]{1,0:T(8,128)(2,1)S(1)}, bf16[64,1024]{1,0:T(8,128)(2,1)S(1)}, u32[]{:S(2)}, u32[]{:S(2)}) collective-permute-start(bf16[64,1024]{1,0:T(8,128)(2,1)S(1)} %get-tuple-element.29), channel_id=1, source_target_pairs={{0,1},{1,2},{2,3},{3,4},{4,5},{5,6},{6,7},{7,8},{8,9},{9,10},{10,1... | collective-permute-start | bytes 393224 | tf_op jit(solution)/shard_map/ppermute | solution.py:296
  32.9 10.3 %collective-permute-start.8 = (bf16[64,1024]{1,0:T(8,128)(2,1)S(1)}, bf16[64,1024]{1,0:T(8,128)(2,1)S(1)}, u32[]{:S(2)}, u32[]{:S(2)}) collective-permute-start(bf16[64,1024]{1,0:T(8,128)(2,1)S(1)} %get-tuple-element.37), channel_id=1, source_target_pairs={{0,240},{1,241},{2,242},{3,243},{4,244},{5,245},{6,246},{7,247},{8... | collective-permute-start | bytes 393224 | tf_op jit(solution)/shard_map/ppermute | solution.py:296
  34.7 8.6 %collective-permute-start.9 = (bf16[64,1024]{1,0:T(8,128)(2,1)S(1)}, bf16[64,1024]{1,0:T(8,128)(2,1)S(1)}, u32[]{:S(2)}, u32[]{:S(2)}) collective-permute-start(bf16[64,1024]{1,0:T(8,128)(2,1)S(1)} %get-tuple-element.38), channel_id=1, source_target_pairs={{0,15},{1,0},{2,1},{3,2},{4,3},{5,4},{6,5},{7,6},{8,7},{9,8},{10,9... | collective-permute-start | bytes 393224 | tf_op jit(solution)/shard_map/ppermute | solution.py:296
  38.9 4.4 %collective-permute-start.7 = (bf16[64,64]{1,0:T(8,128)(2,1)S(1)}, bf16[64,64]{1,0:T(8,128)(2,1)S(1)}, u32[]{:S(2)}, u32[]{:S(2)}) collective-permute-start(bf16[64,64]{1,0:T(8,128)(2,1)S(1)} %get-tuple-element.36), channel_id=1, source_target_pairs={{0,255},{1,240},{2,241},{3,242},{4,243},{5,244},{6,245},{7,246},{8... | collective-permute-start | bytes 24584 | tf_op jit(solution)/shard_map/ppermute | solution.py:296

commit v5 on v4

--- a/solution.py
+++ b/solution.py
@@ -129,12 +129,14 @@
     )
 
 
+def turn_kernel(in_ref, out_ref, rows_ref):
+    to_rows(in_ref[...], rows_ref, out_ref, 0)
+
+
 def forward_kernel(
-    corner_ref, top_ref, left_ref, a_ref, turned_ref,
-    sketched_ref, rightward_ref, tops_ref, first_ref, lwide_ref, second_ref, quad_ref,
-    rows_ref,
+    corner_ref, tops_ref, left_ref, a_ref, turned_ref,
+    sketched_ref, rightward_ref, first_ref, lwide_ref, second_ref, quad_ref,
 ):
-    to_rows(top_ref[...], rows_ref, tops_ref, 0)
     first_ref[...] = dot_nt(tops_ref[...], corner_pair(corner_ref[...])).astype(BF)
     spread(left_ref[...], lwide_ref, 0)
 
@@ -251,13 +253,10 @@
     out_ref[1] = turned[DD:]
 
 
-def finish_kernel(corner_ref, top_ref, left_ref, corner_hbm, top_hbm, left_hbm, sems):
-    copies = [
-        pltpu.make_async_copy(source, target, sems.at[at])
-        for at, (source, target) in enumerate(
-            ((left_ref, left_hbm), (top_ref, top_hbm), (corner_ref, corner_hbm))
-        )
-    ]
+def finish_kernel(*refs):
+    count = len(refs) // 2
+    sems = refs[-1]
+    copies = [pltpu.make_async_copy(refs[at], refs[count + at], sems.at[at]) for at in range(count)]
     for copy in copies:
         copy.start()
     for copy in copies:
@@ -314,15 +313,16 @@
         [pl.BlockSpec(memory_space=pltpu.VMEM), here, here, here],
         room=PREP,
     )(site, in_hbm(sketch), in_hbm(grad_top), in_hbm(grad_left))
-    sketched, rightward, tops, first, lwide, second, quad = call(
+    tops = call(turn_kernel, shape(512, WIDE), [rows], 10**6, 5 * 10**5)(top_used)
+    sketched, rightward, first, lwide, second, quad = call(
         forward_kernel,
         (
             shape(CHI, ORDER), shape(CHI, ORDER),
-            shape(512, WIDE), shape(512, WIDE), shape(WIDE, 2048), shape(256, 4096), shape(512, 2048),
+            shape(512, WIDE), shape(WIDE, 2048), shape(256, 4096), shape(512, 2048),
         ),
-        [rows],
+        [],
         2 * 10**9, 4 * 10**6,
-    )(corner_used, top_used, left_used, a_mat, turned)
+    )(corner_used, tops, left_used, a_mat, turned)
     sketch_beside = from_behind(sketched, 0, -1)
     sketch_below = from_behind(sketched, -1, 0)
     from_left = from_behind(rightward, 0, 1)
@@ -346,14 +346,18 @@
     top_result = from_behind(grad_topped, -1, 0)
     corner_result = from_behind(grad_cornered, -1, -1)
     site_result = call(site_kernel, shape(2, DD, DD, dtype=F32), [], 10**9, 5 * 10**6)(dquad, second, ket, bra)
-    corner_result, top_result, left_result = call(
+    whole = pl.BlockSpec(memory_space=pltpu.VMEM)
+    (left_result,) = call(
+        finish_kernel, (shape(CHI, ORDER),), [pltpu.SemaphoreType.DMA((1,))], 0, 3 * 10**5, [whole], (here,)
+    )(left_result)
+    corner_result, top_result = call(
         finish_kernel,
-        (shape(CHI, CHI), shape(CHI, ORDER), shape(CHI, ORDER)),
-        [pltpu.SemaphoreType.DMA((3,))],
-        0, 6 * 10**5,
-        [pl.BlockSpec(memory_space=pltpu.VMEM)] * 3,
-        (here, here, here),
-    )(corner_result, top_result, left_result)
+        (shape(CHI, CHI), shape(CHI, ORDER)),
+        [pltpu.SemaphoreType.DMA((2,))],
+        0, 3 * 10**5,
+        [whole] * 2,
+        (here, here),
+    )(corner_result, top_result)
     return (
         corner_result[None, None],
         top_result[None, None],

time: 44.4 us -> 44 us (level)
  waiting for transfers between devices: 11.4 us -> 10.3 us
  Pallas kernels: 10.6 us -> 11.3 us
    ppermute x10, waiting for transfers between devices: 11.4 us -> 10.3 us  [from_behind(): return lax.ppermute(value, ('row', 'col'), pairs)]
    pallas_call x1 -> x3, Pallas kernels: 0.73 us -> 1.48 us  [the longest x1 0.68 us: step(): call(finish_kernel, (shape(CHI, CHI), shape(CHI, ORDER)), [pltpu.Semaphor...]
  transfers between devices with their start and end apart: 10 -> 10, of which waited for: 4 -> 5; matrix products, arithmetic and copies ran while one was open for 4% -> 4% of each run, Pallas kernels for 11% -> 15%
where the time goes in v5:
time: 44 us; the launch traced here: 43.9 us
  starting transfers between devices  19.9 us (45%)
  Pallas kernels  11.3 us (26%)
  waiting for transfers between devices  10.3 us (23%)
  local copies, waits for them, and re-layouts  1.58 us (4%)
  between operations  0.88 us (2%)
    ppermute x10, starting transfers between devices, from_behind(): return lax.ppermute(value, ('row', 'col'), pairs)  19.9 us
    ppermute x10, waiting for transfers between devices, from_behind(): return lax.ppermute(value, ('row', 'col'), pairs)  10.3 us
    pallas_call x1, Pallas kernels, step(): call(forward_kernel, (shape(CHI, ORDER), shape(CHI, ORDER), shape(512, WI...  2.21 us
    pallas_call x1, Pallas kernels, step(): call(backward_kernel, (shape(CHI, ORDER), shape(256, 4096), shape(512, 20...  1.81 us
    pallas_call x1, Pallas kernels, step(): call(site_kernel, shape(2, DD, DD, dtype=F32), [], 10 ** 9, 5 * 10 ** 6)  1.55 us
    pallas_call x1, Pallas kernels, step(): call(prepare_kernel, (shape(256, 256), shape(2, 256, 256), shape(2, 256,...  1.46 us
    pallas_call x1, Pallas kernels, step(): call(edges_kernel, (shape(CHI, ORDER), shape(CHI, CHI)), [rows], 3 * 10 *...  1.05 us
  transfers between devices with their start and end apart: 10, of which 5 were waited for; matrix products, arithmetic and copies ran while one was open for 4% of the time, Pallas kernels for 15%

profile of v5, /device:TPU:1, one launch (start us, length us, event | category | flops | bytes accessed | tf_op | source)
XLA Modules:
  0.0 43.9 jit_solution(14225145208533316234)
XLA Ops:
  0.6 2.1 %collective-permute-start.1 = (bf16[64,1024]{1,0:T(8,128)(2,1)}, bf16[64,1024]{1,0:T(8,128)(2,1)S(1)}, u32[]{:S(2)}, u32[]{:S(2)}) collective-permute-start(bf16[64,1024]{1,0:T(8,128)(2,1)} %bitcast.13), channel_id=1, source_target_pairs={{0,16},{1,17},{2,18},{3,19},{4,20},{5,21},{6,22},{7,23},{8,24},{9,... | collective-permute-start | bytes 393224 | tf_op jit(solution)/shard_map/ppermute | solution.py:295
  2.7 3.3 %collective-permute-start.2 = (bf16[64,1024]{1,0:T(8,128)(2,1)}, bf16[64,1024]{1,0:T(8,128)(2,1)S(1)}, u32[]{:S(2)}, u32[]{:S(2)}) collective-permute-start(bf16[64,1024]{1,0:T(8,128)(2,1)} %bitcast.14), channel_id=1, source_target_pairs={{0,1},{1,2},{2,3},{3,4},{4,5},{5,6},{6,7},{7,8},{8,9},{9,10},{10,1... | collective-permute-start | bytes 393224 | tf_op jit(solution)/shard_map/ppermute | solution.py:295
  6.0 0.7 %collective-permute-start = (bf16[64,64]{1,0:T(8,128)(2,1)}, bf16[64,64]{1,0:T(8,128)(2,1)S(1)}, u32[]{:S(2)}, u32[]{:S(2)}) collective-permute-start(bf16[64,64]{1,0:T(8,128)(2,1)} %bitcast.16), channel_id=1, source_target_pairs={{0,17},{1,18},{2,19},{3,20},{4,21},{5,22},{6,23},{7,24},{8,25},{9,... | collective-permute-start | bytes 24584 | tf_op jit(solution)/shard_map/ppermute | solution.py:295
  6.8 0.8 %reshape.14.site_ref = bf16[2,16,16]{2,1,0:T(8,128)(2,1)S(1)} reshape(bf16[1,1,2,4,4,4,4]{6,5,4,3,2,1,0:T(4,128)(2,1)} %param.10) | data formatting | bytes 2048 | tf_op jit(solution)/shard_map/reshape | solution.py:299
  7.6 1.5 %shard_map.103 = (bf16[256,256]{1,0:T(8,128)(2,1)S(1)}, bf16[2,256,256]{2,1,0:T(8,128)(2,1)S(1)}, bf16[2,256,256]{2,1,0:T(8,128)(2,1)S(1)}, bf16[512,256]{1,0:T(...) custom-call(bf16[2,16,16]{2,1,0:T(8,128)(2,1)S(1)} %reshape.14.site_ref, ...), custom_call_target="tpu_custom_call" | custom-call | flops 10000000 | bytes 2000000 | tf_op jit(solution)/shard_map/pallas_call | solution.py:306
  9.1 2.4 %collective-permute-done.1.in_ref = bf16[64,1024]{1,0:T(8,128)(2,1)S(1)} collective-permute-done((bf16[64,1024]{1,0:T(8,128)(2,1)}, bf16[64,1024]{1,0:T(8,128)(2,1)S(1)}, u32[]{:S(2)}, u32[]{:S(2)}) %collective-permute-start.1) | collective-permute-done | bytes 131104 | tf_op jit(solution)/shard_map/ppermute | solution.py:295
  11.4 0.1 shard_map.102.tops_ref
  11.6 1.1 %collective-permute-done.corner_ref = bf16[64,64]{1,0:T(8,128)(2,1)S(1)} collective-permute-done((bf16[64,64]{1,0:T(8,128)(2,1)}, bf16[64,64]{1,0:T(8,128)(2,1)S(1)}, u32[]{:S(2)}, u32[]{:S(2)}) %collective-permute-start) | collective-permute-done | bytes 8224 | tf_op jit(solution)/shard_map/ppermute | solution.py:295
  12.7 0.0 collective-permute-done.2.left_ref
  12.7 2.2 %shard_map.104 = (bf16[64,1024]{1,0:T(8,128)(2,1)S(1)}, bf16[64,1024]{1,0:T(8,128)(2,1)S(1)}, bf16[512,128]{1,0:T(8,128)(2,1)S(1)}, bf16[128,2048]{1,0:T(8,128)(...) custom-call(bf16[64,64]{1,0:T(8,128)(2,1)S(1)} %collective-permute-done.corner_ref, ...), custom_call_target="tpu_custom_call" | custom-call | flops 2000000000 | bytes 4000000 | tf_op jit(solution)/shard_map/pallas_call | solution.py:317
  14.9 3.3 %collective-permute-start.6 = (bf16[64,1024]{1,0:T(8,128)(2,1)S(1)}, bf16[64,1024]{1,0:T(8,128)(2,1)S(1)}, u32[]{:S(2)}, u32[]{:S(2)}) collective-permute-start(bf16[64,1024]{1,0:T(8,128)(2,1)S(1)} %get-tuple-element.28), channel_id=1, source_target_pairs={{0,15},{1,0},{2,1},{3,2},{4,3},{5,4},{6,5},{7,6},{8,7},{9,8},{10,9... | collective-permute-start | bytes 393224 | tf_op jit(solution)/shard_map/ppermute | solution.py:295
  18.2 4.1 %collective-permute-start.5 = (bf16[64,1024]{1,0:T(8,128)(2,1)S(1)}, bf16[64,1024]{1,0:T(8,128)(2,1)S(1)}, u32[]{:S(2)}, u32[]{:S(2)}) collective-permute-start(bf16[64,1024]{1,0:T(8,128)(2,1)S(1)} %get-tuple-element.28), channel_id=1, source_target_pairs={{0,240},{1,241},{2,242},{3,243},{4,244},{5,245},{6,246},{7,247},{8... | collective-permute-start | bytes 393224 | tf_op jit(solution)/shard_map/ppermute | solution.py:295
  22.3 0.8 %shard_map.105 = bf16[64,1024]{1,0:T(8,128)(2,1)S(1)} custom-call(bf16[512,2048]{1,0:T(8,128)(2,1)S(1)} %get-tuple-element.25.quad_ref, bf16[128,2048]{1,0:T(8,128)(2,1)S(1)} %get-tuple-element.26.gwide_ref), custom_call_target="tpu_custom_call" | custom-call | flops 300000000 | bytes 3000000 | tf_op jit(solution)/shard_map/pallas_call | solution.py:329
  23.1 0.1 collective-permute-start.3
  23.2 0.1 collective-permute-start.4
  23.3 0.0 collective-permute-done.6.beside_ref
  23.3 1.7 %collective-permute-done.5.below_ref = bf16[64,1024]{1,0:T(8,128)(2,1)S(1)} collective-permute-done((bf16[64,1024]{1,0:T(8,128)(2,1)S(1)}, bf16[64,1024]{1,0:T(8,128)(2,1)S(1)}, u32[]{:S(2)}, u32[]{:S(2)}) %collective-permute-start.5) | collective-permute-done | bytes 131104 | tf_op jit(solution)/shard_map/ppermute | solution.py:295
  25.1 0.9 %shard_map.106.part_ref = f32[512,2048]{1,0:T(8,128)S(1)} custom-call(bf16[64,1024]{1,0:T(8,128)(2,1)S(1)} %collective-permute-done.5.below_ref, bf16[64,1024]{1,0:T(8,128)(2,1)S(1)} %collective-permute-done.6.beside_ref, bf16[512,256]{1,0:T(8,128)(2,1)S(1)} %get-tuple-element.29.cols_ref, bf16[128,2048]{1,0:T(8,128)(2,1)S(1)} %get-tuple-element.26.gwide_ref), custom_call_target="tpu_custom_call" | custom-call | flops 500000000 | bytes 5000000 | tf_op jit(solution)/shard_map/pallas_call | solution.py:331
  25.9 4.1 %collective-permute-done.3.above_ref = bf16[64,1024]{1,0:T(8,128)(2,1)S(1)} collective-permute-done((bf16[64,1024]{1,0:T(8,128)(2,1)S(1)}, bf16[64,1024]{1,0:T(8,128)(2,1)S(1)}, u32[]{:S(2)}, u32[]{:S(2)}) %collective-permute-start.3) | collective-permute-done | bytes 131104 | tf_op jit(solution)/shard_map/ppermute | solution.py:295
  30.0 0.0 collective-permute-done.4.behind_ref
  30.0 1.8 %shard_map.107 = (bf16[64,1024]{1,0:T(8,128)(2,1)S(1)}, bf16[256,4096]{1,0:T(8,128)(2,1)S(1)}, bf16[512,2048]{1,0:T(8,128)(2,1)S(1)}) custom-call(bf16[64,1024]{1,0:T(8,128)(2,1)S(1)} %collective-permute-done.3.above_ref, bf16[64,1024]{1,0:T(8,128)(2,1)S(1)} %collective-permute-done.4.behind_ref, f32[512,2048]{1,0:T(8,128)S(1)} %shard_map.106.part_ref, ...), custom_call_target="tpu_custom_call" | custom-call | flops 2000000000 | bytes 8000000 | tf_op jit(solution)/shard_map/pallas_call | solution.py:336
  31.8 1.9 %collective-permute-start.9 = (bf16[64,1024]{1,0:T(8,128)(2,1)S(1)}, bf16[64,1024]{1,0:T(8,128)(2,1)S(1)}, u32[]{:S(2)}, u32[]{:S(2)}) collective-permute-start(bf16[64,1024]{1,0:T(8,128)(2,1)S(1)} %get-tuple-element.37), channel_id=1, source_target_pairs={{0,15},{1,0},{2,1},{3,2},{4,3},{5,4},{6,5},{7,6},{8,7},{9,8},{10,9... | collective-permute-start | bytes 393224 | tf_op jit(solution)/shard_map/ppermute | solution.py:295
  33.7 1.1 %shard_map.108 = (bf16[64,1024]{1,0:T(8,128)(2,1)S(1)}, bf16[64,64]{1,0:T(8,128)(2,1)S(1)}) custom-call(bf16[512,2048]{1,0:T(8,128)(2,1)S(1)} %get-tuple-element.31.dsecond_ref, bf16[128,2048]{1,0:T(8,128)(2,1)S(1)} %get-tuple-element.32.lwide_ref, bf16[512,128]{1,0:T(8,128)(2,1)S(1)} %shard_map.102.tops_ref, bf16[64,64]{1,0:T(8,128)(2,1)S(1)} %collective-permute-done.corner_ref), custom_call_target="tpu_custom_call" | custom-call | flops 300000000 | bytes 3000000 | tf_op jit(solution)/shard_map/pallas_call | solution.py:343
  34.8 3.8 %collective-permute-start.8 = (bf16[64,1024]{1,0:T(8,128)(2,1)S(1)}, bf16[64,1024]{1,0:T(8,128)(2,1)S(1)}, u32[]{:S(2)}, u32[]{:S(2)}) collective-permute-start(bf16[64,1024]{1,0:T(8,128)(2,1)S(1)} %get-tuple-element.34), channel_id=1, source_target_pairs={{0,240},{1,241},{2,242},{3,243},{4,244},{5,245},{6,246},{7,247},{8... | collective-permute-start | bytes 393224 | tf_op jit(solution)/shard_map/ppermute | solution.py:295
  38.6 0.4 %collective-permute-start.7 = (bf16[64,64]{1,0:T(8,128)(2,1)S(1)}, bf16[64,64]{1,0:T(8,128)(2,1)S(1)}, u32[]{:S(2)}, u32[]{:S(2)}) collective-permute-start(bf16[64,64]{1,0:T(8,128)(2,1)S(1)} %get-tuple-element.33), channel_id=1, source_target_pairs={{0,255},{1,240},{2,241},{3,242},{4,243},{5,244},{6,245},{7,246},{8... | collective-permute-start | bytes 24584 | tf_op jit(solution)/shard_map/ppermute | solution.py:295
  39.1 1.6 %shard_map.111 = f32[2,16,16]{2,1,0:T(8,128)S(1)} custom-call(bf16[256,4096]{1,0:T(8,128)(2,1)S(1)} %get-tuple-element.38.dquad_ref, bf16[256,4096]{1,0:T(8,128)(2,1)S(1)} %get-tuple-element.39.second_ref, bf16[2,256,256]{2,1,0:T(8,128)(2,1)S(1)} %get-tuple-element.40.ket_ref, bf16[2,256,256]{2,1,0:T(8,128)(2,1)S(1)} %get-tuple-element.41.bra_ref), custom_call_target="tpu_custom_call" | custom-call | flops 1000000000 | bytes 5000000 | tf_op jit(solution)/shard_map/pallas_call | solution.py:348
  40.6 0.7 %reshape.15 = f32[1,1,2,4,4,4,4]{6,5,4,3,2,1,0:T(4,128)} reshape(f32[2,16,16]{2,1,0:T(8,128)S(1)} %shard_map.111) | data formatting | bytes 4096 | tf_op jit(solution)/shard_map/reshape | solution.py:365
  41.4 0.0 collective-permute-done.9.refs_0_
  41.4 0.7 %shard_map.110 = bf16[64,1024]{1,0:T(8,128)(2,1)} custom-call(bf16[64,1024]{1,0:T(8,128)(2,1)S(1)} %collective-permute-done.9.refs_0_), custom_call_target="tpu_custom_call" | custom-call | bytes 300000 | tf_op jit(solution)/shard_map/pallas_call | solution.py:350
  42.0 1.0 %collective-permute-done.7.refs_0_ = bf16[64,64]{1,0:T(8,128)(2,1)S(1)} collective-permute-done((bf16[64,64]{1,0:T(8,128)(2,1)S(1)}, bf16[64,64]{1,0:T(8,128)(2,1)S(1)}, u32[]{:S(2)}, u32[]{:S(2)}) %collective-permute-start.7) | collective-permute-done | bytes 8224 | tf_op jit(solution)/shard_map/ppermute | solution.py:295
  43.0 0.0 collective-permute-done.8.refs_1_
  43.0 0.7 %shard_map.109 = (bf16[64,64]{1,0:T(8,128)(2,1)}, bf16[64,1024]{1,0:T(8,128)(2,1)}) custom-call(bf16[64,64]{1,0:T(8,128)(2,1)S(1)} %collective-permute-done.7.refs_0_, bf16[64,1024]{1,0:T(8,128)(2,1)S(1)} %collective-permute-done.8.refs_1_), custom_call_target="tpu_custom_call" | custom-call | bytes 300000 | tf_op jit(solution)/shard_map/pallas_call | solution.py:353
Async XLA Ops:
  0.6 10.8 %collective-permute-start.1 = (bf16[64,1024]{1,0:T(8,128)(2,1)}, bf16[64,1024]{1,0:T(8,128)(2,1)S(1)}, u32[]{:S(2)}, u32[]{:S(2)}) collective-permute-start(bf16[64,1024]{1,0:T(8,128)(2,1)} %bitcast.13), channel_id=1, source_target_pairs={{0,16},{1,17},{2,18},{3,19},{4,20},{5,21},{6,22},{7,23},{8,24},{9,... | collective-permute-start | bytes 393224 | tf_op jit(solution)/shard_map/ppermute | solution.py:295
  2.7 10.0 %collective-permute-start.2 = (bf16[64,1024]{1,0:T(8,128)(2,1)}, bf16[64,1024]{1,0:T(8,128)(2,1)S(1)}, u32[]{:S(2)}, u32[]{:S(2)}) collective-permute-start(bf16[64,1024]{1,0:T(8,128)(2,1)} %bitcast.14), channel_id=1, source_target_pairs={{0,1},{1,2},{2,3},{3,4},{4,5},{5,6},{6,7},{7,8},{8,9},{9,10},{10,1... | collective-permute-start | bytes 393224 | tf_op jit(solution)/shard_map/ppermute | solution.py:295
  6.0 6.7 %collective-permute-start = (bf16[64,64]{1,0:T(8,128)(2,1)}, bf16[64,64]{1,0:T(8,128)(2,1)S(1)}, u32[]{:S(2)}, u32[]{:S(2)}) collective-permute-start(bf16[64,64]{1,0:T(8,128)(2,1)} %bitcast.16), channel_id=1, source_target_pairs={{0,17},{1,18},{2,19},{3,20},{4,21},{5,22},{6,23},{7,24},{8,25},{9,... | collective-permute-start | bytes 24584 | tf_op jit(solution)/shard_map/ppermute | solution.py:295
  14.9 8.4 %collective-permute-start.6 = (bf16[64,1024]{1,0:T(8,128)(2,1)S(1)}, bf16[64,1024]{1,0:T(8,128)(2,1)S(1)}, u32[]{:S(2)}, u32[]{:S(2)}) collective-permute-start(bf16[64,1024]{1,0:T(8,128)(2,1)S(1)} %get-tuple-element.28), channel_id=1, source_target_pairs={{0,15},{1,0},{2,1},{3,2},{4,3},{5,4},{6,5},{7,6},{8,7},{9,8},{10,9... | collective-permute-start | bytes 393224 | tf_op jit(solution)/shard_map/ppermute | solution.py:295
  18.2 6.8 %collective-permute-start.5 = (bf16[64,1024]{1,0:T(8,128)(2,1)S(1)}, bf16[64,1024]{1,0:T(8,128)(2,1)S(1)}, u32[]{:S(2)}, u32[]{:S(2)}) collective-permute-start(bf16[64,1024]{1,0:T(8,128)(2,1)S(1)} %get-tuple-element.28), channel_id=1, source_target_pairs={{0,240},{1,241},{2,242},{3,243},{4,244},{5,245},{6,246},{7,247},{8... | collective-permute-start | bytes 393224 | tf_op jit(solution)/shard_map/ppermute | solution.py:295
  23.1 6.9 %collective-permute-start.3 = (bf16[64,1024]{1,0:T(8,128)(2,1)S(1)}, bf16[64,1024]{1,0:T(8,128)(2,1)S(1)}, u32[]{:S(2)}, u32[]{:S(2)}) collective-permute-start(bf16[64,1024]{1,0:T(8,128)(2,1)S(1)} %shard_map.105), channel_id=1, source_target_pairs={{0,16},{1,17},{2,18},{3,19},{4,20},{5,21},{6,22},{7,23},{8,24},{9,... | collective-permute-start | bytes 393224 | tf_op jit(solution)/shard_map/ppermute | solution.py:295
  23.2 6.8 %collective-permute-start.4 = (bf16[64,1024]{1,0:T(8,128)(2,1)S(1)}, bf16[64,1024]{1,0:T(8,128)(2,1)S(1)}, u32[]{:S(2)}, u32[]{:S(2)}) collective-permute-start(bf16[64,1024]{1,0:T(8,128)(2,1)S(1)} %get-tuple-element.27), channel_id=1, source_target_pairs={{0,1},{1,2},{2,3},{3,4},{4,5},{5,6},{6,7},{7,8},{8,9},{9,10},{10,1... | collective-permute-start | bytes 393224 | tf_op jit(solution)/shard_map/ppermute | solution.py:295
  31.8 9.6 %collective-permute-start.9 = (bf16[64,1024]{1,0:T(8,128)(2,1)S(1)}, bf16[64,1024]{1,0:T(8,128)(2,1)S(1)}, u32[]{:S(2)}, u32[]{:S(2)}) collective-permute-start(bf16[64,1024]{1,0:T(8,128)(2,1)S(1)} %get-tuple-element.37), channel_id=1, source_target_pairs={{0,15},{1,0},{2,1},{3,2},{4,3},{5,4},{6,5},{7,6},{8,7},{9,8},{10,9... | collective-permute-start | bytes 393224 | tf_op jit(solution)/shard_map/ppermute | solution.py:295
  34.8 8.2 %collective-permute-start.8 = (bf16[64,1024]{1,0:T(8,128)(2,1)S(1)}, bf16[64,1024]{1,0:T(8,128)(2,1)S(1)}, u32[]{:S(2)}, u32[]{:S(2)}) collective-permute-start(bf16[64,1024]{1,0:T(8,128)(2,1)S(1)} %get-tuple-element.34), channel_id=1, source_target_pairs={{0,240},{1,241},{2,242},{3,243},{4,244},{5,245},{6,246},{7,247},{8... | collective-permute-start | bytes 393224 | tf_op jit(solution)/shard_map/ppermute | solution.py:295
  38.6 4.4 %collective-permute-start.7 = (bf16[64,64]{1,0:T(8,128)(2,1)S(1)}, bf16[64,64]{1,0:T(8,128)(2,1)S(1)}, u32[]{:S(2)}, u32[]{:S(2)}) collective-permute-start(bf16[64,64]{1,0:T(8,128)(2,1)S(1)} %get-tuple-element.33), channel_id=1, source_target_pairs={{0,255},{1,240},{2,241},{3,242},{4,243},{5,244},{6,245},{7,246},{8... | collective-permute-start | bytes 24584 | tf_op jit(solution)/shard_map/ppermute | solution.py:295
